TPU v7x, 32 devices: a whole 2x2x4 slice. The times are simulated.
32 devices in a mesh: row: 8 (over z, x), col: 4 (over y, core).
Axes of the slice: x: 2, y: 2, z: 4, core: 2. Of those that a mesh axis runs over, the one named last changes fastest.
Arguments:
- hamiltonian: float32 [18432, 18432], P('row', 'col'), may hold values from -6 to 6, as said below
- panel: float32 [18432, 128], P(('row', 'col')), may hold values from -0.03125 to 0.03125
Outputs:
- updated: float32 [18432, 18432], P('row', 'col')
Inputs may be any that keep to these rules, and one draw needn't show every extreme that they name: `hamiltonian`: H is symmetric: the entry at stored row p and stored column q equals the entry whose stored row and column stand for the two global indices swapped.
All inputs are finite; a program needn't handle non-finite values.
Results may differ from a plain program's by a relative error of at most 0.0002.
Values sent between devices are 32-bit elements; how exact they have to be, the bound alone decides.
No kernel may reach another device: no remote copies, remote signals or barrier semaphores. Data moves between devices by JAX's collectives and lax.ppermute only.
A program may use at most 192 MiB of HBM per device.

v0:
```python
import functools

import jax
import jax.numpy as jnp
from jax import lax
from jax.experimental import pallas as pl
from jax.experimental.pallas import tpu as pltpu
from jax.sharding import PartitionSpec as P


B = 128
BOTH = ("row", "col")
HIGHEST = lax.Precision.HIGHEST
NT = (((1,), (1,)), ((), ()))


def matmul(left, right):
    return jnp.dot(left, right, precision=HIGHEST, preferred_element_type=jnp.float32)


def shape_panel(panel_raw, global_rows, block_width):
    global_block = (global_rows // block_width)[:, None]
    within = (global_rows % block_width)[:, None]
    column_ids = jnp.arange(panel_raw.shape[1], dtype=jnp.int32)[None, :]
    unit_block = jnp.where(
        column_ids < within, panel_raw, jnp.where(column_ids == within, 1.0, 0.0)
    )
    kept = jnp.where(global_block == 1, unit_block, 0.0)
    return jnp.where(global_block >= 2, panel_raw, kept)


def upper_inverse(gram_matrix):
    width = gram_matrix.shape[0]
    identity_matrix = jnp.eye(width, dtype=gram_matrix.dtype)
    diagonal_half = jnp.sum(gram_matrix * identity_matrix, axis=1) * 0.5
    nilpotent = jnp.triu(gram_matrix, 1) / diagonal_half[:, None]
    power = -nilpotent
    result = identity_matrix + power
    for _ in range(width.bit_length()):
        power = matmul(power, power)
        result = matmul(result, identity_matrix + power)
    diagonal_row = jnp.sum(gram_matrix * identity_matrix, axis=0) * 0.5
    return result / diagonal_row[None, :]


def halves(x):
    high = x.astype(jnp.bfloat16)
    low = (x - high.astype(jnp.float32)).astype(jnp.bfloat16)
    return high, low


def beside(*arrays):
    return jnp.concatenate(arrays, axis=1)


def group_of(blocks, sizes):
    return next(g for g in sizes if blocks % g == 0)


def in_vmem(x):
    return pltpu.with_memory_space_constraint(x, pltpu.VMEM)


def product_kernel(
    groups, width, per_step, cols, here_ref, h_ref, v_ref, kept_ref, own_ref, other_ref, gram_ref,
    total, inner, sems,
):
    step, steps = pl.program_id(0), pl.num_programs(0)
    tile = groups * width * per_step
    ahead = min(2, sems.shape[0])

    def copy(k):
        at = pl.ds(pl.multiple_of(k * tile, tile), tile)
        return pltpu.make_async_copy(h_ref.at[:, at], kept_ref.at[:, at], sems.at[k])

    @pl.when(step == 0)
    def _():
        for k in range(ahead):
            copy(k).start()
        total[...] = jnp.zeros_like(total)
        inner[...] = jnp.zeros_like(inner)

    parts = []
    for i in range(per_step):
        for s in range(groups):
            parts.append(beside(*halves(v_ref[s, i * width : (i + 1) * width, :])))
    right = jnp.concatenate(parts, axis=0)
    inner[...] += lax.dot_general(
        right, right, (((0,), (0,)), ((), ())), preferred_element_type=jnp.float32
    )

    @pl.when(step + ahead < steps)
    def _():
        copy(step + ahead).start()

    copy(step).wait()
    high, low = halves(kept_ref[:, pl.ds(pl.multiple_of(step * tile, tile), tile)])
    total[...] += jnp.dot(
        high, right, preferred_element_type=jnp.float32
    ) + jnp.dot(low, right, preferred_element_type=jnp.float32)

    @pl.when(step == steps - 1)
    def _():
        half = inner[:, :width] + inner[:, width:]
        gram_ref[...] = half[:width] + half[width:]
        size = own_ref.shape[1]
        pairs = cols // 2
        hi, core = here_ref[0], here_ref[1]
        for k in range(pairs):
            at = (k + pairs - hi) % pairs
            for c in range(2):
                rows = slice((2 * k + c) * size, (2 * k + c + 1) * size)
                value = total[rows, :width] + total[rows, width:]

                @pl.when(core == c)
                def _():
                    own_ref[at] = value

                @pl.when(core != c)
                def _():
                    other_ref[at] = value


def product(h, v, cols, here):
    rows, columns = h.shape
    groups, group_rows, width = v.shape
    per_step = group_of(group_rows // width, (3, 2, 1))
    tile = groups * per_step * width
    half = (cols // 2, rows // cols, width)
    steps = columns // tile
    return pl.pallas_call(
        functools.partial(product_kernel, groups, width, per_step, cols),
        out_shape=[
            pltpu.VMEM(h.shape, h.dtype),
            jax.ShapeDtypeStruct(half, jnp.float32),
            jax.ShapeDtypeStruct(half, jnp.float32),
            jax.ShapeDtypeStruct((width, width), jnp.float32),
        ],
        grid=(steps,),
        in_specs=[
            pl.BlockSpec(memory_space=pltpu.SMEM),
            pl.BlockSpec(memory_space=pl.ANY),
            pl.BlockSpec((groups, per_step * width, width), lambda k: (0, k, 0)),
        ],
        out_specs=[
            pl.BlockSpec(memory_space=pltpu.VMEM),
            pl.BlockSpec(half, lambda k: (0, 0, 0)),
            pl.BlockSpec(half, lambda k: (0, 0, 0)),
            pl.BlockSpec((width, width), lambda k: (0, 0)),
        ],
        scratch_shapes=[
            pltpu.VMEM((rows, 2 * width), jnp.float32),
            pltpu.VMEM((2 * width, 2 * width), jnp.float32),
            pltpu.SemaphoreType.DMA((steps,)),
        ],
        compiler_params=pltpu.CompilerParams(
            dimension_semantics=("arbitrary",), vmem_limit_bytes=20 << 20
        ),
        cost_estimate=pl.CostEstimate(
            flops=8 * rows * columns * width,
            bytes_accessed=4 * rows * columns,
            transcendentals=0,
        ),
        name="panel_product",
    )(here, h, v)


def update_kernel(
    groups, width, per_step, parts, *refs
):
    h_refs = refs[:parts]
    vr_ref, pr_ref, vc_ref, pc_ref, mix_ref, out_ref, left, mix = refs[parts:]
    step = pl.program_id(0)

    def y_of(p, v):
        p_high, p_low = halves(p)
        v_high, v_low = halves(v)
        y = jnp.dot(
            beside(p_high, v_high, p_high, v_high, p_low, v_low),
            mix[...],
            preferred_element_type=jnp.float32,
        )
        return halves(y), (v_high, v_low)

    @pl.when(step == 0)
    def _():
        high, low = halves(mix_ref[...])
        size = high.shape[0]
        mix[:size] = high
        mix[size : 2 * size] = low
        mix[2 * size :] = high
        for r in range(0, out_ref.shape[0], width):
            at = slice(r, r + width)
            (y_high, y_low), (v_high, v_low) = y_of(pr_ref[at, :], vr_ref[at, :])
            left[at, :] = beside(v_high, y_high, v_high, y_high, v_low, y_low)

    parts = []
    for i in range(per_step):
        for s in range(groups):
            at = slice(i * width, (i + 1) * width)
            (y_high, y_low), (v_high, v_low) = y_of(pc_ref[s, at, :], vc_ref[s, at, :])
            parts.append(beside(y_high, v_high, y_low, v_low, y_high, v_high))
    right = jnp.concatenate(parts, axis=0)
    tile = out_ref.shape[1]
    at = pl.ds(pl.multiple_of(step * tile, tile), tile)
    size = out_ref.shape[0] // 2
    for k in range(2):
        rows = slice(k * size, (k + 1) * size)
        out_ref[rows, :] = h_refs[0][rows, at] - lax.dot_general(
            left[rows, :], right, NT, preferred_element_type=jnp.float32
        )


def update(held, v_rows, p_rows, v_cols, p_cols, mix):
    rows, columns = sum(h.shape[0] for h in held), held[0].shape[1]
    groups, group_rows, width = v_cols.shape
    per_step = group_of(group_rows // width, (2, 3, 1))
    tile = groups * per_step * width
    whole = lambda shape: pl.BlockSpec(
        shape, lambda k: (0,) * len(shape), pipeline_mode=pl.Buffered(1)
    )
    piece = pl.BlockSpec((groups, per_step * width, width), lambda k: (0, k, 0))
    return pl.pallas_call(
        functools.partial(update_kernel, groups, width, per_step, len(held)),
        out_shape=jax.ShapeDtypeStruct((rows, columns), jnp.float32),
        grid=(columns // tile,),
        in_specs=[
            *[pl.BlockSpec(memory_space=pltpu.VMEM)] * len(held),
            whole((rows, width)),
            whole((rows, width)),
            piece,
            piece,
            whole((2 * width, width)),
        ],
        out_specs=pl.BlockSpec((rows, tile), lambda k: (0, k)),
        scratch_shapes=[
            pltpu.VMEM((rows, 6 * width), jnp.bfloat16),
            pltpu.VMEM((6 * width, width), jnp.bfloat16),
        ],
        compiler_params=pltpu.CompilerParams(
            dimension_semantics=("arbitrary",), vmem_limit_bytes=20 << 20
        ),
        cost_estimate=pl.CostEstimate(
            flops=12 * rows * columns * width,
            bytes_accessed=8 * rows * columns,
            transcendentals=0,
        ),
        name="rank_update",
    )(*map(in_vmem, held), v_rows, p_rows, v_cols, p_cols, mix)


class Place:
    def __init__(self):
        self.rows = lax.axis_size("row")
        self.cols = lax.axis_size("col")
        self.row = lax.axis_index("row")
        self.col = lax.axis_index("col")
        self.pairs = self.cols // 2
        n = self.rows
        self.places = {d: self.ring_at(d) for d in range(-(n // 2), n // 2 + 1)}
        hi, core = self.col // 2, self.col % 2
        self.same_core = [(hi - d) % self.pairs * 2 + core for d in range(self.pairs)]
        self.other = [(hi - d) % self.pairs * 2 + 1 - core for d in range(self.pairs)]
        self.here = jnp.stack([hi, core]).astype(jnp.int32)

    def before(self, x):
        known = (self.places, self.same_core, self.other, self.here)
        known, x = lax.optimization_barrier((known, x))
        self.places, self.same_core, self.other, self.here = known
        return x

    def to_shard(self, x, shift):
        route = []
        for g in range(self.rows):
            for c in range(self.cols):
                piece = (c // 2 + shift) % self.pairs * 2 + c % 2
                target = g // self.cols * self.cols + piece
                route.append((g * self.cols + c, target * self.cols + g % self.cols))
        return lax.ppermute(x, BOTH, route)

    def other_core(self, x):
        return lax.ppermute(x, "col", [(c, c ^ 1) for c in range(self.cols)])

    def along_pairs(self, x, shift):
        n = self.pairs
        return lax.ppermute(
            x, "col", [(c, (c // 2 + shift) % n * 2 + c % 2) for c in range(self.cols)]
        )

    def ring(self, x, shift):
        n = self.rows
        order = list(range(0, n, 2)) + list(range(1, n, 2))[::-1]
        return lax.ppermute(
            x, "row", [(order[i], order[(i + shift) % n]) for i in range(n)]
        )

    def ring_at(self, shift):
        n = self.rows
        r = self.row
        here = jnp.where(r % 2 == 0, r // 2, n - 1 - r // 2)
        there = (here - shift) % n
        return jnp.where(there < n // 2, 2 * there, 2 * (n - there) - 1)

    def gather_ring(self, shard, asides=(), held=None):
        n = self.rows
        half = shard.shape[0] // 16 * 8
        asides = list(asides) + [lambda seen: None] * n
        held = {} if held is None else held
        held[0] = ahead = back = shard
        for d in range(1, n // 2 + 1):
            if d == n // 2:
                ahead, back = ahead[:half], back[half:]
            seen = ahead
            held[d] = ahead = self.ring(ahead, 1)
            held[-d] = back = self.ring(back, -1)
            asides[d - 1](seen)
        out = jnp.zeros((n,) + shard.shape, shard.dtype)
        for d, x in held.items():
            start = half if d == -(n // 2) else 0
            out = put(out, x, self.places[d], start)
        return out

    def sum_col(self, x):
        total = x
        for bit in range(1, self.cols):
            total = total + lax.ppermute(x, "col", [(c, c ^ bit) for c in range(self.cols)])
        return total

    def sum_bit(self, x, bit):
        n = self.rows
        return x + lax.ppermute(x, "row", [(r, r ^ bit) for r in range(n)])


def put(out, x, at, start=0):
    return lax.dynamic_update_slice(
        out, x[None], (at, start, 0), allow_negative_indices=False
    )


def after(x, seen):
    return lax.optimization_barrier((x, seen))[0]


class ColGather:
    def __init__(self, place, piece):
        self.place, self.piece = place, piece

    def first(self, seen):
        self.piece = after(self.piece, seen)
        self.mine = [self.piece] + [
            self.place.along_pairs(self.piece, d) for d in range(1, self.place.pairs)
        ]

    def second(self, seen):
        place = self.place
        self.mine = [after(x, seen) for x in self.mine]
        self.theirs = [place.other_core(x) for x in self.mine]

    def rows(self):
        place = self.place
        out = jnp.zeros((place.cols,) + self.piece.shape, self.piece.dtype)
        for d in range(place.pairs):
            out = put(out, self.mine[d], place.same_core[d])
            out = put(out, self.theirs[d], place.other[d])
        return out.reshape(-1, self.piece.shape[1])


def step(hamiltonian, panel):
    place = Place()
    width = panel.shape[1]
    piece_rows = panel.shape[0]
    groups = place.rows // place.cols
    position = place.col * piece_rows + jnp.arange(piece_rows, dtype=jnp.int32)
    global_rows = (position // B * place.rows + place.row) * B + position % B
    piece = place.before(shape_panel(panel, global_rows, B))

    sums = {}

    def add_bit(name, bit):
        def run(seen):
            if bit < place.rows:
                sums[name] = place.sum_bit(after(sums[name], seen), bit)

        return run

    def both(*runs):
        def run(seen):
            for r in runs:
                r(seen)

        return run

    levels = place.rows.bit_length() - 1
    v_shard = place.to_shard(piece, 0)
    v_gather = ColGather(place, piece)
    v_cols = place.gather_ring(v_shard, (v_gather.first, lambda seen: None, v_gather.second))
    v_cols = v_cols.reshape(groups, -1, width)
    v_rows = v_gather.rows()
    kept, own, other, gram = product(hamiltonian, v_cols, place.cols, place.here)

    mine = own + place.other_core(other)
    p_shard = place.to_shard(mine[0], 0)
    for d in range(1, place.pairs):
        p_shard = p_shard + place.to_shard(mine[d], d)
    v_mine = [v_gather.mine[-d % place.pairs] for d in range(place.pairs)]
    cross = sum(matmul(v_mine[d].T, mine[d]) for d in range(place.pairs))
    sums["cross"] = place.sum_col(cross)
    gram = place.sum_col(after(gram, mine))
    block_factor = upper_inverse(gram)

    def own_piece(seen):
        own = mine[0]
        for d in range(1, place.pairs):
            own = own + place.along_pairs(after(mine[d], seen), d)
        sums["gather"] = ColGather(place, own)

    p_cols = place.gather_ring(
        p_shard,
        (
            both(add_bit("cross", 1), own_piece),
            both(add_bit("cross", 2), lambda seen: sums["gather"].first(seen)),
            both(add_bit("cross", 4), lambda seen: sums["gather"].second(seen)),
            *(add_bit("cross", 1 << k) for k in range(3, levels)),
        ),
    ).reshape(groups, -1, width)
    middle = matmul(matmul(block_factor.T, sums["cross"]), block_factor)
    mix = jnp.concatenate([block_factor, -0.5 * middle], axis=0)
    return update(
        [kept], v_rows, sums["gather"].rows(), v_cols, p_cols, mix
    )


def solution(mesh):
    return jax.shard_map(
        step,
        mesh=mesh,
        in_specs=(P("row", "col"), P(("row", "col"), None)),
        out_specs=P("row", "col"),
        check_vma=False,
    )
```

profile of v0, /device:TPU:0, one launch (start us, length us, event | category | flops | bytes accessed | tf_op | source)
XLA Modules:
  0.0 167.6 jit_solution(2298270889704090142)
XLA Ops:
  0.8 2.0 %select_select_fusion = f32[576,128]{1,0:T(8,128)} fusion(f32[576,128]{1,0:T(8,128)} %param.3, s32[576]{0:T(1024)S(1)} %add_select_fusion, pred[576]{0:T(1024)(128)(4,1)S(1)} %get-tuple-element.73, pred[576]{0:T(1024)(128)(4,1)S(1)} %get-tuple-element.72), kind=kLoop, calls=%fused_computation.27 | loop fusion | flops 442368 | bytes 593280 | tf_op jit(solution)/shard_map/jit(_where)/select_n | solution.py:29
  2.7 1.6 collective-permute-start
  4.3 10.9 %collective-permute-start.2 = (f32[576,128]{1,0:T(8,128)S(1)}, f32[576,128]{1,0:T(8,128)S(1)}, u32[]{:S(2)}, u32[]{:S(2)}) collective-permute-start(f32[576,128]{1,0:T(8,128)S(1)} %collective-permute-done), channel_id=1, source_target_pairs={{0,4},{8,0},{16,8},{24,16},{28,24},{20,28},{12,20},{4,12},{1,5},{9... | collective-permute-start | bytes 884744 | tf_op jit(solution)/shard_map/ppermute | solution.py:293
  15.2 3.3 %collective-permute-start.1 = (f32[576,128]{1,0:T(8,128)S(1)}, f32[576,128]{1,0:T(8,128)S(1)}, u32[]{:S(2)}, u32[]{:S(2)}) collective-permute-start(f32[576,128]{1,0:T(8,128)S(1)} %collective-permute-done), channel_id=1, source_target_pairs={{0,8},{8,16},{16,24},{24,28},{28,20},{20,12},{12,4},{4,0},{1,9},{9... | collective-permute-start | bytes 884744 | tf_op jit(solution)/shard_map/ppermute | solution.py:293
  18.5 2.0 %collective-permute-start.10 = (f32[576,128]{1,0:T(8,128)}, f32[576,128]{1,0:T(8,128)}, u32[]{:S(2)}, u32[]{:S(2)}) collective-permute-start(f32[576,128]{1,0:T(8,128)} %select_select_fusion), channel_id=1, source_target_pairs={{0,2},{1,3},{2,0},{3,1},{4,6},{5,7},{6,4},{7,5},{8,10},{9,11},{10,... | collective-permute-start | bytes 884744 | tf_op jit(solution)/shard_map/ppermute | solution.py:286
  20.7 5.0 %collective-permute-done.2 = f32[576,128]{1,0:T(8,128)S(1)} collective-permute-done((f32[576,128]{1,0:T(8,128)S(1)}, f32[576,128]{1,0:T(8,128)S(1)}, u32[]{:S(2)}, u32[]{:S(2)}) %collective-permute-start.2) | collective-permute-done | bytes 294944 | tf_op jit(solution)/shard_map/ppermute | solution.py:293
  25.7 2.0 %collective-permute-start.3 = (f32[576,128]{1,0:T(8,128)S(1)}, f32[576,128]{1,0:T(8,128)S(1)}, u32[]{:S(2)}, u32[]{:S(2)}) collective-permute-start(f32[576,128]{1,0:T(8,128)S(1)} %collective-permute-done.1), channel_id=1, source_target_pairs={{0,8},{8,16},{16,24},{24,28},{28,20},{20,12},{12,4},{4,0},{1,9},{9... | collective-permute-start | bytes 884744 | tf_op jit(solution)/shard_map/ppermute | solution.py:293
  27.8 6.3 %collective-permute-done.3 = f32[576,128]{1,0:T(8,128)S(1)} collective-permute-done((f32[576,128]{1,0:T(8,128)S(1)}, f32[576,128]{1,0:T(8,128)S(1)}, u32[]{:S(2)}, u32[]{:S(2)}) %collective-permute-start.3) | collective-permute-done | bytes 294944 | tf_op jit(solution)/shard_map/ppermute | solution.py:293
  34.6 1.7 %collective-permute-start.5 = (f32[576,128]{1,0:T(8,128)S(1)}, f32[576,128]{1,0:T(8,128)S(1)}, u32[]{:S(2)}, u32[]{:S(2)}) collective-permute-start(f32[576,128]{1,0:T(8,128)S(1)} %collective-permute-done.3), channel_id=1, source_target_pairs={{0,8},{8,16},{16,24},{24,28},{28,20},{20,12},{12,4},{4,0},{1,9},{9... | collective-permute-start | bytes 884744 | tf_op jit(solution)/shard_map/ppermute | solution.py:293
  37.8 8.3 %collective-permute-done.6 = f32[576,128]{1,0:T(8,128)S(1)} collective-permute-done((f32[576,128]{1,0:T(8,128)S(1)}, f32[576,128]{1,0:T(8,128)S(1)}, u32[]{:S(2)}, u32[]{:S(2)}) %collective-permute-start.6) | collective-permute-done | bytes 294944 | tf_op jit(solution)/shard_map/ppermute | solution.py:293
  46.5 1.8 %collective-permute-start.7 = (f32[288,128]{1,0:T(8,128)S(1)}, f32[288,128]{1,0:T(8,128)S(1)}, u32[]{:S(2)}, u32[]{:S(2)}) collective-permute-start(f32[288,128]{1,0:T(8,128)S(1)} %slice.28), channel_id=1, source_target_pairs={{0,8},{8,16},{16,24},{24,28},{28,20},{20,12},{12,4},{4,0},{1,9},{9... | collective-permute-start | bytes 442376 | tf_op jit(solution)/shard_map/ppermute | solution.py:293
  48.3 3.3 %collective-permute-done.7 = f32[288,128]{1,0:T(8,128)S(1)} collective-permute-done((f32[288,128]{1,0:T(8,128)S(1)}, f32[288,128]{1,0:T(8,128)S(1)}, u32[]{:S(2)}, u32[]{:S(2)}) %collective-permute-start.7) | collective-permute-done | bytes 147488 | tf_op jit(solution)/shard_map/ppermute | solution.py:293
  53.1 20.6 %panel_product.1 = (f32[2304,4608]{1,0:T(8,128)S(1)}, f32[2,576,128]{2,1,0:T(8,128)}, f32[2,576,128]{2,1,0:T(8,128)}, f32[128,128]{1,0:T(8,128)}) custom-call(s32[2]{0:T(128)} %pad_add_fusion.here_ref, f32[2304,4608]{1,0:T(8,128)} %h_ref.1, f32[2,2304,128]{2,1,0:T(8,128)} %bitcast.93), custom_call_target="tpu_custom_call" | custom-call | flops 10871635968 | bytes 42467328 | tf_op jit(solution)/shard_map/panel_product/pallas_call | solution.py:131
  76.9 1.6 add.260
  78.4 1.7 fusion.24
  82.3 1.7 convolution_add_fusion.1
  83.9 1.6 collective-permute-start.32
  87.0 4.1 %collective-permute-start.14 = (f32[576,128]{1,0:T(8,128)S(1)}, f32[576,128]{1,0:T(8,128)S(1)}, u32[]{:S(2)}, u32[]{:S(2)}) collective-permute-start(f32[576,128]{1,0:T(8,128)S(1)} %get-tuple-element.56), channel_id=1, source_target_pairs={{0,8},{1,12},{2,0},{3,4},{4,9},{5,13},{6,1},{7,5},{8,10},{9,14},{1... | collective-permute-start | bytes 884744 | tf_op jit(solution)/shard_map/ppermute | solution.py:279
  94.7 4.7 %collective-permute-done.14 = f32[576,128]{1,0:T(8,128)S(1)} collective-permute-done((f32[576,128]{1,0:T(8,128)S(1)}, f32[576,128]{1,0:T(8,128)S(1)}, u32[]{:S(2)}, u32[]{:S(2)}) %collective-permute-start.14) | collective-permute-done | bytes 294944 | tf_op jit(solution)/shard_map/ppermute | solution.py:279
  99.5 1.8 %collective-permute-start.16 = (f32[576,128]{1,0:T(8,128)S(1)}, f32[576,128]{1,0:T(8,128)S(1)}, u32[]{:S(2)}, u32[]{:S(2)}) collective-permute-start(f32[576,128]{1,0:T(8,128)S(1)} %get-tuple-element.69), channel_id=1, source_target_pairs={{0,8},{8,16},{16,24},{24,28},{28,20},{20,12},{12,4},{4,0},{1,9},{9... | collective-permute-start | bytes 884744 | tf_op jit(solution)/shard_map/ppermute | solution.py:293
  101.4 1.8 %collective-permute-start.21 = (f32[576,128]{1,0:T(8,128)S(1)}, f32[576,128]{1,0:T(8,128)S(1)}, u32[]{:S(2)}, u32[]{:S(2)}) collective-permute-start(f32[576,128]{1,0:T(8,128)S(1)} %get-tuple-element.69), channel_id=1, source_target_pairs={{0,4},{8,0},{16,8},{24,16},{28,24},{20,28},{12,20},{4,12},{1,5},{9... | collective-permute-start | bytes 884744 | tf_op jit(solution)/shard_map/ppermute | solution.py:293
  103.2 1.9 %collective-permute-start.33 = (f32[128,128]{1,0:T(8,128)S(1)}, f32[128,128]{1,0:T(8,128)S(1)}, u32[]{:S(2)}, u32[]{:S(2)}) collective-permute-start(f32[128,128]{1,0:T(8,128)S(1)} %add_add_fusion), channel_id=1, source_target_pairs={{0,4},{4,0},{8,12},{12,8},{16,20},{20,16},{24,28},{28,24},{1,5},{5... | collective-permute-start | bytes 196616 | tf_op jit(solution)/shard_map/ppermute | solution.py:331
  105.3 5.2 %collective-permute-done.33 = f32[128,128]{1,0:T(8,128)S(1)} collective-permute-done((f32[128,128]{1,0:T(8,128)S(1)}, f32[128,128]{1,0:T(8,128)S(1)}, u32[]{:S(2)}, u32[]{:S(2)}) %collective-permute-start.33) | collective-permute-done | bytes 65568 | tf_op jit(solution)/shard_map/ppermute | solution.py:331
  111.7 1.7 %collective-permute-start.19 = (f32[576,128]{1,0:T(8,128)S(1)}, f32[576,128]{1,0:T(8,128)S(1)}, u32[]{:S(2)}, u32[]{:S(2)}) collective-permute-start(f32[576,128]{1,0:T(8,128)S(1)} %fusion.25), channel_id=1, source_target_pairs={{0,2},{1,3},{2,0},{3,1},{4,6},{5,7},{6,4},{7,5},{8,10},{9,11},{10,... | collective-permute-start | bytes 884744 | tf_op jit(solution)/shard_map/ppermute | solution.py:286
  113.7 1.8 %collective-permute-start.22 = (f32[576,128]{1,0:T(8,128)S(1)}, f32[576,128]{1,0:T(8,128)S(1)}, u32[]{:S(2)}, u32[]{:S(2)}) collective-permute-start(f32[576,128]{1,0:T(8,128)S(1)} %collective-permute-done.21), channel_id=1, source_target_pairs={{0,4},{8,0},{16,8},{24,16},{28,24},{20,28},{12,20},{4,12},{1,5},{9... | collective-permute-start | bytes 884744 | tf_op jit(solution)/shard_map/ppermute | solution.py:293
  115.6 5.5 %collective-permute-done.17 = f32[576,128]{1,0:T(8,128)S(1)} collective-permute-done((f32[576,128]{1,0:T(8,128)S(1)}, f32[576,128]{1,0:T(8,128)S(1)}, u32[]{:S(2)}, u32[]{:S(2)}) %collective-permute-start.17) | collective-permute-done | bytes 294944 | tf_op jit(solution)/shard_map/ppermute | solution.py:293
  121.0 1.8 %collective-permute-start.35 = (f32[128,128]{1,0:T(8,128)S(1)}, f32[128,128]{1,0:T(8,128)S(1)}, u32[]{:S(2)}, u32[]{:S(2)}) collective-permute-start(f32[128,128]{1,0:T(8,128)S(1)} %add.280), channel_id=1, source_target_pairs={{0,16},{4,20},{8,24},{12,28},{16,0},{20,4},{24,8},{28,12},{1,17},{... | collective-permute-start | bytes 196616 | tf_op jit(solution)/shard_map/ppermute | solution.py:331
  123.3 1.9 %collective-permute-start.23 = (f32[576,128]{1,0:T(8,128)S(1)}, f32[576,128]{1,0:T(8,128)S(1)}, u32[]{:S(2)}, u32[]{:S(2)}) collective-permute-start(f32[576,128]{1,0:T(8,128)S(1)} %collective-permute-done.17), channel_id=1, source_target_pairs={{0,8},{8,16},{16,24},{24,28},{28,20},{20,12},{12,4},{4,0},{1,9},{9... | collective-permute-start | bytes 884744 | tf_op jit(solution)/shard_map/ppermute | solution.py:293
  128.1 6.0 %collective-permute-done.24 = f32[576,128]{1,0:T(8,128)S(1)} collective-permute-done((f32[576,128]{1,0:T(8,128)S(1)}, f32[576,128]{1,0:T(8,128)S(1)}, u32[]{:S(2)}, u32[]{:S(2)}) %collective-permute-start.24) | collective-permute-done | bytes 294944 | tf_op jit(solution)/shard_map/ppermute | solution.py:293
  134.5 2.0 %collective-permute-start.25 = (f32[288,128]{1,0:T(8,128)S(1)}, f32[288,128]{1,0:T(8,128)S(1)}, u32[]{:S(2)}, u32[]{:S(2)}) collective-permute-start(f32[288,128]{1,0:T(8,128)S(1)} %slice.32), channel_id=1, source_target_pairs={{0,8},{8,16},{16,24},{24,28},{28,20},{20,12},{12,4},{4,0},{1,9},{9... | collective-permute-start | bytes 442376 | tf_op jit(solution)/shard_map/ppermute | solution.py:293
  136.6 3.3 %collective-permute-done.25 = f32[288,128]{1,0:T(8,128)S(1)} collective-permute-done((f32[288,128]{1,0:T(8,128)S(1)}, f32[288,128]{1,0:T(8,128)S(1)}, u32[]{:S(2)}, u32[]{:S(2)}) %collective-permute-start.25) | collective-permute-done | bytes 147488 | tf_op jit(solution)/shard_map/ppermute | solution.py:293
  141.4 26.3 %rank_update.1 = f32[2304,4608]{1,0:T(8,128)} custom-call(f32[2304,4608]{1,0:T(8,128)S(1)} %get-tuple-element.46.refs_0_, f32[2304,128]{1,0:T(8,128)} %bitcast.97, f32[2304,128]{1,0:T(8,128)} %bitcast.96, f32[2,2304,128]{2,1,0:T(8,128)} %bitcast.94, f32[2,2304,128]{2,1,0:T(8,128)} %bitcast.95, f32[256,128]{1,0:T(8,128)} %pad_maximum_fusion.refs_5_), custom_call_target="tpu_custom_call" | custom-call | flops 16307453952 | bytes 84934656 | tf_op jit(solution)/shard_map/rank_update/pallas_call | solution.py:223
  (120 shorter events, 21.9 us)
Async XLA Ops:
  4.3 21.3 %collective-permute-start.2 = (f32[576,128]{1,0:T(8,128)S(1)}, f32[576,128]{1,0:T(8,128)S(1)}, u32[]{:S(2)}, u32[]{:S(2)}) collective-permute-start(f32[576,128]{1,0:T(8,128)S(1)} %collective-permute-done), channel_id=1, source_target_pairs={{0,4},{8,0},{16,8},{24,16},{28,24},{20,28},{12,20},{4,12},{1,5},{9... | collective-permute-start | bytes 884744 | tf_op jit(solution)/shard_map/ppermute | solution.py:293
  15.2 10.4 %collective-permute-start.1 = (f32[576,128]{1,0:T(8,128)S(1)}, f32[576,128]{1,0:T(8,128)S(1)}, u32[]{:S(2)}, u32[]{:S(2)}) collective-permute-start(f32[576,128]{1,0:T(8,128)S(1)} %collective-permute-done), channel_id=1, source_target_pairs={{0,8},{8,16},{16,24},{24,28},{28,20},{20,12},{12,4},{4,0},{1,9},{9... | collective-permute-start | bytes 884744 | tf_op jit(solution)/shard_map/ppermute | solution.py:293
  18.5 9.2 %collective-permute-start.10 = (f32[576,128]{1,0:T(8,128)}, f32[576,128]{1,0:T(8,128)}, u32[]{:S(2)}, u32[]{:S(2)}) collective-permute-start(f32[576,128]{1,0:T(8,128)} %select_select_fusion), channel_id=1, source_target_pairs={{0,2},{1,3},{2,0},{3,1},{4,6},{5,7},{6,4},{7,5},{8,10},{9,11},{10,... | collective-permute-start | bytes 884744 | tf_op jit(solution)/shard_map/ppermute | solution.py:286
  25.6 11.8 %collective-permute-start.4 = (f32[576,128]{1,0:T(8,128)S(1)}, f32[576,128]{1,0:T(8,128)S(1)}, u32[]{:S(2)}, u32[]{:S(2)}) collective-permute-start(f32[576,128]{1,0:T(8,128)S(1)} %collective-permute-done.2), channel_id=1, source_target_pairs={{0,4},{8,0},{16,8},{24,16},{28,24},{20,28},{12,20},{4,12},{1,5},{9... | collective-permute-start | bytes 884744 | tf_op jit(solution)/shard_map/ppermute | solution.py:293
  25.7 8.4 %collective-permute-start.3 = (f32[576,128]{1,0:T(8,128)S(1)}, f32[576,128]{1,0:T(8,128)S(1)}, u32[]{:S(2)}, u32[]{:S(2)}) collective-permute-start(f32[576,128]{1,0:T(8,128)S(1)} %collective-permute-done.1), channel_id=1, source_target_pairs={{0,8},{8,16},{16,24},{24,28},{28,20},{20,12},{12,4},{4,0},{1,9},{9... | collective-permute-start | bytes 884744 | tf_op jit(solution)/shard_map/ppermute | solution.py:293
  34.1 39.8 %collective-permute-start.9 = (f32[576,128]{1,0:T(8,128)}, f32[576,128]{1,0:T(8,128)}, u32[]{:S(2)}, u32[]{:S(2)}) collective-permute-start(f32[576,128]{1,0:T(8,128)} %select_select_fusion), channel_id=1, source_target_pairs={{0,1},{1,0},{2,3},{3,2},{4,5},{5,4},{6,7},{7,6},{8,9},{9,8},{10,11... | collective-permute-start | bytes 884744 | tf_op jit(solution)/shard_map/ppermute | solution.py:282
  34.1 41.8 %collective-permute-start.11 = (f32[576,128]{1,0:T(8,128)}, f32[576,128]{1,0:T(8,128)}, u32[]{:S(2)}, u32[]{:S(2)}) collective-permute-start(f32[576,128]{1,0:T(8,128)} %collective-permute-done.10), channel_id=1, source_target_pairs={{0,1},{1,0},{2,3},{3,2},{4,5},{5,4},{6,7},{7,6},{8,9},{9,8},{10,11... | collective-permute-start | bytes 884744 | tf_op jit(solution)/shard_map/ppermute | solution.py:282
  34.6 11.9 %collective-permute-start.5 = (f32[576,128]{1,0:T(8,128)S(1)}, f32[576,128]{1,0:T(8,128)S(1)}, u32[]{:S(2)}, u32[]{:S(2)}) collective-permute-start(f32[576,128]{1,0:T(8,128)S(1)} %collective-permute-done.3), channel_id=1, source_target_pairs={{0,8},{8,16},{16,24},{24,28},{28,20},{20,12},{12,4},{4,0},{1,9},{9... | collective-permute-start | bytes 884744 | tf_op jit(solution)/shard_map/ppermute | solution.py:293
  37.4 8.7 %collective-permute-start.6 = (f32[576,128]{1,0:T(8,128)S(1)}, f32[576,128]{1,0:T(8,128)S(1)}, u32[]{:S(2)}, u32[]{:S(2)}) collective-permute-start(f32[576,128]{1,0:T(8,128)S(1)} %collective-permute-done.4), channel_id=1, source_target_pairs={{0,4},{8,0},{16,8},{24,16},{28,24},{20,28},{12,20},{4,12},{1,5},{9... | collective-permute-start | bytes 884744 | tf_op jit(solution)/shard_map/ppermute | solution.py:293
  46.1 5.6 %collective-permute-start.8 = (f32[288,128]{1,0:T(8,128)S(1)}, f32[288,128]{1,0:T(8,128)S(1)}, u32[]{:S(2)}, u32[]{:S(2)}) collective-permute-start(f32[288,128]{1,0:T(8,128)S(1)} %slice.29), channel_id=1, source_target_pairs={{0,4},{8,0},{16,8},{24,16},{28,24},{20,28},{12,20},{4,12},{1,5},{9... | collective-permute-start | bytes 442376 | tf_op jit(solution)/shard_map/ppermute | solution.py:293
  46.5 5.2 %collective-permute-start.7 = (f32[288,128]{1,0:T(8,128)S(1)}, f32[288,128]{1,0:T(8,128)S(1)}, u32[]{:S(2)}, u32[]{:S(2)}) collective-permute-start(f32[288,128]{1,0:T(8,128)S(1)} %slice.28), channel_id=1, source_target_pairs={{0,8},{8,16},{16,24},{24,28},{28,20},{20,12},{12,4},{4,0},{1,9},{9... | collective-permute-start | bytes 442376 | tf_op jit(solution)/shard_map/ppermute | solution.py:293
  80.1 6.1 %collective-permute-start.29 = (f32[128,128]{1,0:T(8,128)S(1)}, f32[128,128]{1,0:T(8,128)S(1)}, u32[]{:S(2)}, u32[]{:S(2)}) collective-permute-start(f32[128,128]{1,0:T(8,128)S(1)} %copy-done.4), channel_id=1, source_target_pairs={{0,3},{1,2},{2,1},{3,0},{4,7},{5,6},{6,5},{7,4},{8,11},{9,10},{10,... | collective-permute-start | bytes 196616 | tf_op jit(solution)/shard_map/ppermute | solution.py:326
  83.9 10.7 %collective-permute-start.32 = (f32[128,128]{1,0:T(8,128)S(1)}, f32[128,128]{1,0:T(8,128)S(1)}, u32[]{:S(2)}, u32[]{:S(2)}) collective-permute-start(f32[128,128]{1,0:T(8,128)S(1)} %convolution_add_fusion.1), channel_id=1, source_target_pairs={{0,3},{1,2},{2,1},{3,0},{4,7},{5,6},{6,5},{7,4},{8,11},{9,10},{10,... | collective-permute-start | bytes 196616 | tf_op jit(solution)/shard_map/ppermute | solution.py:326
  85.5 9.1 %collective-permute-start.31 = (f32[128,128]{1,0:T(8,128)S(1)}, f32[128,128]{1,0:T(8,128)S(1)}, u32[]{:S(2)}, u32[]{:S(2)}) collective-permute-start(f32[128,128]{1,0:T(8,128)S(1)} %convolution_add_fusion.1), channel_id=1, source_target_pairs={{0,2},{1,3},{2,0},{3,1},{4,6},{5,7},{6,4},{7,5},{8,10},{9,11},{10,... | collective-permute-start | bytes 196616 | tf_op jit(solution)/shard_map/ppermute | solution.py:326
  86.2 8.4 %collective-permute-start.30 = (f32[128,128]{1,0:T(8,128)S(1)}, f32[128,128]{1,0:T(8,128)S(1)}, u32[]{:S(2)}, u32[]{:S(2)}) collective-permute-start(f32[128,128]{1,0:T(8,128)S(1)} %convolution_add_fusion.1), channel_id=1, source_target_pairs={{0,1},{1,0},{2,3},{3,2},{4,5},{5,4},{6,7},{7,6},{8,9},{9,8},{10,11... | collective-permute-start | bytes 196616 | tf_op jit(solution)/shard_map/ppermute | solution.py:326
  86.3 8.4 %collective-permute-start.13 = (f32[576,128]{1,0:T(8,128)S(1)}, f32[576,128]{1,0:T(8,128)S(1)}, u32[]{:S(2)}, u32[]{:S(2)}) collective-permute-start(f32[576,128]{1,0:T(8,128)S(1)} %get-tuple-element.70), channel_id=1, source_target_pairs={{0,0},{1,4},{2,8},{3,12},{4,1},{5,5},{6,9},{7,13},{8,2},{9,6},{10,... | collective-permute-start | bytes 884744 | tf_op jit(solution)/shard_map/ppermute | solution.py:279
  87.0 12.3 %collective-permute-start.14 = (f32[576,128]{1,0:T(8,128)S(1)}, f32[576,128]{1,0:T(8,128)S(1)}, u32[]{:S(2)}, u32[]{:S(2)}) collective-permute-start(f32[576,128]{1,0:T(8,128)S(1)} %get-tuple-element.56), channel_id=1, source_target_pairs={{0,8},{1,12},{2,0},{3,4},{4,9},{5,13},{6,1},{7,5},{8,10},{9,14},{1... | collective-permute-start | bytes 884744 | tf_op jit(solution)/shard_map/ppermute | solution.py:279
  99.5 11.0 %collective-permute-start.16 = (f32[576,128]{1,0:T(8,128)S(1)}, f32[576,128]{1,0:T(8,128)S(1)}, u32[]{:S(2)}, u32[]{:S(2)}) collective-permute-start(f32[576,128]{1,0:T(8,128)S(1)} %get-tuple-element.69), channel_id=1, source_target_pairs={{0,8},{8,16},{16,24},{24,28},{28,20},{20,12},{12,4},{4,0},{1,9},{9... | collective-permute-start | bytes 884744 | tf_op jit(solution)/shard_map/ppermute | solution.py:293
  101.4 9.2 %collective-permute-start.15 = (f32[576,128]{1,0:T(8,128)S(1)}, f32[576,128]{1,0:T(8,128)S(1)}, u32[]{:S(2)}, u32[]{:S(2)}) collective-permute-start(f32[576,128]{1,0:T(8,128)S(1)} %get-tuple-element.56), channel_id=1, source_target_pairs={{0,2},{1,3},{2,0},{3,1},{4,6},{5,7},{6,4},{7,5},{8,10},{9,11},{10,... | collective-permute-start | bytes 884744 | tf_op jit(solution)/shard_map/ppermute | solution.py:286
  101.4 12.3 %collective-permute-start.21 = (f32[576,128]{1,0:T(8,128)S(1)}, f32[576,128]{1,0:T(8,128)S(1)}, u32[]{:S(2)}, u32[]{:S(2)}) collective-permute-start(f32[576,128]{1,0:T(8,128)S(1)} %get-tuple-element.69), channel_id=1, source_target_pairs={{0,4},{8,0},{16,8},{24,16},{28,24},{20,28},{12,20},{4,12},{1,5},{9... | collective-permute-start | bytes 884744 | tf_op jit(solution)/shard_map/ppermute | solution.py:293
  103.2 7.3 %collective-permute-start.33 = (f32[128,128]{1,0:T(8,128)S(1)}, f32[128,128]{1,0:T(8,128)S(1)}, u32[]{:S(2)}, u32[]{:S(2)}) collective-permute-start(f32[128,128]{1,0:T(8,128)S(1)} %add_add_fusion), channel_id=1, source_target_pairs={{0,4},{4,0},{8,12},{12,8},{16,20},{20,16},{24,28},{28,24},{1,5},{5... | collective-permute-start | bytes 196616 | tf_op jit(solution)/shard_map/ppermute | solution.py:331
  110.6 4.9 %collective-permute-start.34 = (f32[128,128]{1,0:T(8,128)S(1)}, f32[128,128]{1,0:T(8,128)S(1)}, u32[]{:S(2)}, u32[]{:S(2)}) collective-permute-start(f32[128,128]{1,0:T(8,128)S(1)} %add.279), channel_id=1, source_target_pairs={{0,8},{4,12},{8,0},{12,4},{16,24},{20,28},{24,16},{28,20},{1,9},{5... | collective-permute-start | bytes 196616 | tf_op jit(solution)/shard_map/ppermute | solution.py:331
  111.7 9.3 %collective-permute-start.19 = (f32[576,128]{1,0:T(8,128)S(1)}, f32[576,128]{1,0:T(8,128)S(1)}, u32[]{:S(2)}, u32[]{:S(2)}) collective-permute-start(f32[576,128]{1,0:T(8,128)S(1)} %fusion.25), channel_id=1, source_target_pairs={{0,2},{1,3},{2,0},{3,1},{4,6},{5,7},{6,4},{7,5},{8,10},{9,11},{10,... | collective-permute-start | bytes 884744 | tf_op jit(solution)/shard_map/ppermute | solution.py:286
  113.5 7.6 %collective-permute-start.17 = (f32[576,128]{1,0:T(8,128)S(1)}, f32[576,128]{1,0:T(8,128)S(1)}, u32[]{:S(2)}, u32[]{:S(2)}) collective-permute-start(f32[576,128]{1,0:T(8,128)S(1)} %collective-permute-done.16), channel_id=1, source_target_pairs={{0,8},{8,16},{16,24},{24,28},{28,20},{20,12},{12,4},{4,0},{1,9},{9... | collective-permute-start | bytes 884744 | tf_op jit(solution)/shard_map/ppermute | solution.py:293
  113.7 11.7 %collective-permute-start.22 = (f32[576,128]{1,0:T(8,128)S(1)}, f32[576,128]{1,0:T(8,128)S(1)}, u32[]{:S(2)}, u32[]{:S(2)}) collective-permute-start(f32[576,128]{1,0:T(8,128)S(1)} %collective-permute-done.21), channel_id=1, source_target_pairs={{0,4},{8,0},{16,8},{24,16},{28,24},{20,28},{12,20},{4,12},{1,5},{9... | collective-permute-start | bytes 884744 | tf_op jit(solution)/shard_map/ppermute | solution.py:293
  121.0 5.9 %collective-permute-start.35 = (f32[128,128]{1,0:T(8,128)S(1)}, f32[128,128]{1,0:T(8,128)S(1)}, u32[]{:S(2)}, u32[]{:S(2)}) collective-permute-start(f32[128,128]{1,0:T(8,128)S(1)} %add.280), channel_id=1, source_target_pairs={{0,16},{4,20},{8,24},{12,28},{16,0},{20,4},{24,8},{28,12},{1,17},{... | collective-permute-start | bytes 196616 | tf_op jit(solution)/shard_map/ppermute | solution.py:331
  122.8 11.6 %collective-permute-start.18 = (f32[576,128]{1,0:T(8,128)S(1)}, f32[576,128]{1,0:T(8,128)S(1)}, u32[]{:S(2)}, u32[]{:S(2)}) collective-permute-start(f32[576,128]{1,0:T(8,128)S(1)} %fusion.25), channel_id=1, source_target_pairs={{0,1},{1,0},{2,3},{3,2},{4,5},{5,4},{6,7},{7,6},{8,9},{9,8},{10,11... | collective-permute-start | bytes 884744 | tf_op jit(solution)/shard_map/ppermute | solution.py:282
  122.8 13.8 %collective-permute-start.20 = (f32[576,128]{1,0:T(8,128)S(1)}, f32[576,128]{1,0:T(8,128)S(1)}, u32[]{:S(2)}, u32[]{:S(2)}) collective-permute-start(f32[576,128]{1,0:T(8,128)S(1)} %collective-permute-done.19), channel_id=1, source_target_pairs={{0,1},{1,0},{2,3},{3,2},{4,5},{5,4},{6,7},{7,6},{8,9},{9,8},{10,11... | collective-permute-start | bytes 884744 | tf_op jit(solution)/shard_map/ppermute | solution.py:282
  123.3 11.2 %collective-permute-start.23 = (f32[576,128]{1,0:T(8,128)S(1)}, f32[576,128]{1,0:T(8,128)S(1)}, u32[]{:S(2)}, u32[]{:S(2)}) collective-permute-start(f32[576,128]{1,0:T(8,128)S(1)} %collective-permute-done.17), channel_id=1, source_target_pairs={{0,8},{8,16},{16,24},{24,28},{28,20},{20,12},{12,4},{4,0},{1,9},{9... | collective-permute-start | bytes 884744 | tf_op jit(solution)/shard_map/ppermute | solution.py:293
  125.4 8.7 %collective-permute-start.24 = (f32[576,128]{1,0:T(8,128)S(1)}, f32[576,128]{1,0:T(8,128)S(1)}, u32[]{:S(2)}, u32[]{:S(2)}) collective-permute-start(f32[576,128]{1,0:T(8,128)S(1)} %collective-permute-done.22), channel_id=1, source_target_pairs={{0,4},{8,0},{16,8},{24,16},{28,24},{20,28},{12,20},{4,12},{1,5},{9... | collective-permute-start | bytes 884744 | tf_op jit(solution)/shard_map/ppermute | solution.py:293
  134.1 5.8 %collective-permute-start.26 = (f32[288,128]{1,0:T(8,128)S(1)}, f32[288,128]{1,0:T(8,128)S(1)}, u32[]{:S(2)}, u32[]{:S(2)}) collective-permute-start(f32[288,128]{1,0:T(8,128)S(1)} %slice.33), channel_id=1, source_target_pairs={{0,4},{8,0},{16,8},{24,16},{28,24},{20,28},{12,20},{4,12},{1,5},{9... | collective-permute-start | bytes 442376 | tf_op jit(solution)/shard_map/ppermute | solution.py:293
  134.5 5.4 %collective-permute-start.25 = (f32[288,128]{1,0:T(8,128)S(1)}, f32[288,128]{1,0:T(8,128)S(1)}, u32[]{:S(2)}, u32[]{:S(2)}) collective-permute-start(f32[288,128]{1,0:T(8,128)S(1)} %slice.32), channel_id=1, source_target_pairs={{0,8},{8,16},{16,24},{24,28},{28,20},{20,12},{12,4},{4,0},{1,9},{9... | collective-permute-start | bytes 442376 | tf_op jit(solution)/shard_map/ppermute | solution.py:293
  (9 other events, 41.3 us)
where the time goes:
time: 168 us
  starting transfers between devices  50.9 us (30%)
  waiting for transfers between devices  49 us (29%)
  Pallas kernels  46.9 us (28%)
  local copies, waits for them, and re-layouts  7.83 us (5%)
  matrix products  7.23 us (4%)
  other arithmetic  5.13 us (3%)
    ppermute x16, waiting for transfers between devices, ring(): lax.ppermute(x, 'row', [(order[i], order[(i + shift) % n]) for i in range...  37.7 us
    ppermute x16, starting transfers between devices, ring(): lax.ppermute(x, 'row', [(order[i], order[(i + shift) % n]) for i in range...  30.5 us
    pallas_call x1, Pallas kernels, update(): pl.pallas_call(functools.partial(update_kernel, groups, width, per_step,...  26.3 us
    pallas_call x1, Pallas kernels, product(): pl.pallas_call(functools.partial(product_kernel, groups, width, per_step,...  20.6 us
    dot_general x20, matrix products, matmul(): jnp.dot(left, right, precision=HIGHEST, preferred_element_type=jnp.float32)  7.23 us
    ppermute x3, waiting for transfers between devices, sum_bit(): return x + lax.ppermute(x, 'row', [(r, r ^ bit) for r in range(n)])  6.55 us
    ppermute x3, starting transfers between devices, to_shard(): return lax.ppermute(x, BOTH, route)  6.42 us
    ppermute x3, starting transfers between devices, sum_bit(): return x + lax.ppermute(x, 'row', [(r, r ^ bit) for r in range(n)])  4.74 us
  transfers between devices with their start and end apart: 36, of which 10 were waited for; matrix products, arithmetic and copies ran while one was open for 7% of the time, Pallas kernels for 12%

commit v1 on v0

--- a/solution.py
+++ b/solution.py
@@ -203,8 +203,8 @@
     right = jnp.concatenate(parts, axis=0)
     tile = out_ref.shape[1]
     at = pl.ds(pl.multiple_of(step * tile, tile), tile)
-    size = out_ref.shape[0] // 2
-    for k in range(2):
+    size = out_ref.shape[0] // 4
+    for k in range(4):
         rows = slice(k * size, (k + 1) * size)
         out_ref[rows, :] = h_refs[0][rows, at] - lax.dot_general(
             left[rows, :], right, NT, preferred_element_type=jnp.float32
@@ -238,7 +238,7 @@
             pltpu.VMEM((6 * width, width), jnp.bfloat16),
         ],
         compiler_params=pltpu.CompilerParams(
-            dimension_semantics=("arbitrary",), vmem_limit_bytes=20 << 20
+            dimension_semantics=("arbitrary",), vmem_limit_bytes=18 << 20
         ),
         cost_estimate=pl.CostEstimate(
             flops=12 * rows * columns * width,
@@ -301,34 +301,37 @@
         there = (here - shift) % n
         return jnp.where(there < n // 2, 2 * there, 2 * (n - there) - 1)
 
-    def gather_ring(self, shard, asides=(), held=None):
+    def gather_ring(self, shard, asides=()):
         n = self.rows
         half = shard.shape[0] // 16 * 8
         asides = list(asides) + [lambda seen: None] * n
-        held = {} if held is None else held
-        held[0] = ahead = back = shard
+        held = [(shard, 0, 0)]
+        ahead = back = (shard[:half], shard[half:])
         for d in range(1, n // 2 + 1):
-            if d == n // 2:
-                ahead, back = ahead[:half], back[half:]
-            seen = ahead
-            held[d] = ahead = self.ring(ahead, 1)
-            held[-d] = back = self.ring(back, -1)
+            seen = ahead[0]
+            if d < n // 2:
+                moved = [(self.ring(a, 1), self.ring(b, -1)) for a, b in zip(ahead, back)]
+                ahead, back = zip(*moved)
+                for k, start in ((0, 0), (1, half)):
+                    held += [(ahead[k], d, start), (back[k], -d, start)]
+            else:
+                held.append((self.ring(ahead[0], 1), d, 0))
+                held.append((self.ring(back[1], -1), d, half))
             asides[d - 1](seen)
         out = jnp.zeros((n,) + shard.shape, shard.dtype)
-        for d, x in held.items():
-            start = half if d == -(n // 2) else 0
+        for x, d, start in held:
             out = put(out, x, self.places[d], start)
         return out
 
-    def sum_col(self, x):
-        total = x
-        for bit in range(1, self.cols):
-            total = total + lax.ppermute(x, "col", [(c, c ^ bit) for c in range(self.cols)])
-        return total
-
-    def sum_bit(self, x, bit):
+    def all_col(self, x):
+        return [x] + [
+            lax.ppermute(x, "col", [(c, c ^ bit) for c in range(self.cols)])
+            for bit in range(1, self.cols)
+        ]
+
+    def other_bit(self, x, bit):
         n = self.rows
-        return x + lax.ppermute(x, "row", [(r, r ^ bit) for r in range(n)])
+        return lax.ppermute(x, "row", [(r, r ^ bit) for r in range(n)])
 
 
 def put(out, x, at, start=0):
@@ -356,8 +359,11 @@
         self.mine = [after(x, seen) for x in self.mine]
         self.theirs = [place.other_core(x) for x in self.mine]
 
-    def rows(self):
+    def rows(self, seen=None):
         place = self.place
+        if seen is not None:
+            self.mine = [after(x, seen) for x in self.mine]
+            self.theirs = [after(x, seen) for x in self.theirs]
         out = jnp.zeros((place.cols,) + self.piece.shape, self.piece.dtype)
         for d in range(place.pairs):
             out = put(out, self.mine[d], place.same_core[d])
@@ -379,7 +385,8 @@
     def add_bit(name, bit):
         def run(seen):
             if bit < place.rows:
-                sums[name] = place.sum_bit(after(sums[name], seen), bit)
+                x = after(sum(sums[name]), seen)
+                sums[name] = (x, place.other_bit(x, bit))
 
         return run
 
@@ -390,12 +397,10 @@
 
         return run
 
-    levels = place.rows.bit_length() - 1
     v_shard = place.to_shard(piece, 0)
     v_gather = ColGather(place, piece)
     v_cols = place.gather_ring(v_shard, (v_gather.first, lambda seen: None, v_gather.second))
     v_cols = v_cols.reshape(groups, -1, width)
-    v_rows = v_gather.rows()
     kept, own, other, gram = product(hamiltonian, v_cols, place.cols, place.here)
 
     mine = own + place.other_core(other)
@@ -404,29 +409,42 @@
         p_shard = p_shard + place.to_shard(mine[d], d)
     v_mine = [v_gather.mine[-d % place.pairs] for d in range(place.pairs)]
     cross = sum(matmul(v_mine[d].T, mine[d]) for d in range(place.pairs))
-    sums["cross"] = place.sum_col(cross)
-    gram = place.sum_col(after(gram, mine))
-    block_factor = upper_inverse(gram)
+    grams = place.all_col(after(gram, mine))
+    sums["cross"] = place.all_col(cross)
+    block_factor = upper_inverse(sum(grams))
 
     def own_piece(seen):
-        own = mine[0]
-        for d in range(1, place.pairs):
-            own = own + place.along_pairs(after(mine[d], seen), d)
-        sums["gather"] = ColGather(place, own)
+        sums["own"] = [mine[0]] + [
+            place.along_pairs(after(mine[d], seen), d) for d in range(1, place.pairs)
+        ]
+
+    def gather_first(seen):
+        sums["gather"] = ColGather(place, sum(sums["own"]))
+        sums["gather"].first(seen)
+        sums["v_rows"] = v_gather.rows(seen)
+
+    def skip(seen):
+        return None
+
+    def gather_second(seen):
+        sums["gather"].second(seen)
 
     p_cols = place.gather_ring(
         p_shard,
         (
             both(add_bit("cross", 1), own_piece),
-            both(add_bit("cross", 2), lambda seen: sums["gather"].first(seen)),
-            both(add_bit("cross", 4), lambda seen: sums["gather"].second(seen)),
-            *(add_bit("cross", 1 << k) for k in range(3, levels)),
+            both(add_bit("cross", 2), gather_first),
+            add_bit("cross", 4),
+            *(
+                both(add_bit("cross", 1 << k), gather_second if k == 3 else skip)
+                for k in range(3, place.rows // 2)
+            ),
         ),
     ).reshape(groups, -1, width)
-    middle = matmul(matmul(block_factor.T, sums["cross"]), block_factor)
+    middle = matmul(matmul(block_factor.T, sum(sums["cross"])), block_factor)
     mix = jnp.concatenate([block_factor, -0.5 * middle], axis=0)
     return update(
-        [kept], v_rows, sums["gather"].rows(), v_cols, p_cols, mix
+        [kept], sums["v_rows"], sums["gather"].rows(), v_cols, p_cols, mix
     )
 
 

time: 168 us -> 168 us (level)
  starting transfers between devices: 50.9 us -> 57.9 us
  local copies, waits for them, and re-layouts: 7.83 us -> 4.32 us
  matrix products: 7.23 us -> 5.31 us
    ppermute x16 -> x28, waiting for transfers between devices: 37.7 us -> 25.4 us  [ring(): lax.ppermute(x, 'row', [(order[i], order[(i + shift) % n]) for i in range...]
    ppermute x16 -> x28, starting transfers between devices: 30.5 us -> 40.7 us  [ring(): lax.ppermute(x, 'row', [(order[i], order[(i + shift) % n]) for i in range...]
    ppermute x3, waiting for transfers between devices: 0.01 us -> 10.1 us  [along_pairs(): lax.ppermute(x, 'col', [(c, (c // 2 + shift) % n * 2 + c % 2) for c in ra...]
    dynamic_update_slice x25 -> x37, local copies, waits for them, and re-layouts: 4.45 us -> 0.69 us  [put(): lax.dynamic_update_slice(out, x[None], (at, start, 0), allow_negative_ind...]
    ppermute x9, waiting for transfers between devices: 6.56 us -> 9.93 us  [the longest x3 5.02 us: other_bit(): return lax.ppermute(x, 'row', [(r, r ^ bit) for r in range(n)])]
    ppermute x9, starting transfers between devices: 9.2 us -> 6.6 us  [the longest x6 3.56 us: all_col(): lax.ppermute(x, 'col', [(c, c ^ bit) for c in range(self.cols)])]
    dot_general x20, matrix products: 7.23 us -> 5.31 us  [matmul(): jnp.dot(left, right, precision=HIGHEST, preferred_element_type=jnp.float32)]
    ppermute x3, waiting for transfers between devices: 4.67 us -> 2.93 us  [to_shard(): return lax.ppermute(x, BOTH, route)]
  transfers between devices with their start and end apart: 36 -> 48, of which waited for: 10 -> 22; matrix products, arithmetic and copies ran while one was open for 7% -> 4% of each run, Pallas kernels for 12% -> 0%
where the time goes in v1:
time: 168 us; the launch traced here: 167 us
  starting transfers between devices  57.9 us (34%)
  waiting for transfers between devices  48.3 us (29%)
  Pallas kernels  46.8 us (28%)
  matrix products  5.31 us (3%)
  local copies, waits for them, and re-layouts  4.32 us (3%)
  other arithmetic  3.92 us (2%)
    ppermute x28, starting transfers between devices, ring(): lax.ppermute(x, 'row', [(order[i], order[(i + shift) % n]) for i in range...  40.7 us
    pallas_call x1, Pallas kernels, update(): pl.pallas_call(functools.partial(update_kernel, groups, width, per_step,...  26.2 us
    ppermute x28, waiting for transfers between devices, ring(): lax.ppermute(x, 'row', [(order[i], order[(i + shift) % n]) for i in range...  25.4 us
    pallas_call x1, Pallas kernels, product(): pl.pallas_call(functools.partial(product_kernel, groups, width, per_step,...  20.6 us
    ppermute x3, waiting for transfers between devices, along_pairs(): lax.ppermute(x, 'col', [(c, (c // 2 + shift) % n * 2 + c % 2) for c in ra...  10.1 us
    dot_general x20, matrix products, matmul(): jnp.dot(left, right, precision=HIGHEST, preferred_element_type=jnp.float32)  5.31 us
    ppermute x3, starting transfers between devices, to_shard(): return lax.ppermute(x, BOTH, route)  5.12 us
    ppermute x3, waiting for transfers between devices, other_bit(): return lax.ppermute(x, 'row', [(r, r ^ bit) for r in range(n)])  5.02 us
  transfers between devices with their start and end apart: 48, of which 22 were waited for; matrix products, arithmetic and copies ran while one was open for 4% of the time, Pallas kernels for 0%

profile of v1, /device:TPU:0, one launch (start us, length us, event | category | flops | bytes accessed | tf_op | source)
XLA Modules:
  0.0 167.4 jit_solution(1446031740389610682)
XLA Ops:
  0.7 1.3 select_select_fusion
  2.7 11.7 %collective-permute-start.4 = (f32[288,128]{1,0:T(8,128)S(1)}, f32[288,128]{1,0:T(8,128)S(1)}, u32[]{:S(2)}, u32[]{:S(2)}) collective-permute-start(f32[288,128]{1,0:T(8,128)S(1)} %get-tuple-element.80), channel_id=1, source_target_pairs={{0,4},{8,0},{16,8},{24,16},{28,24},{20,28},{12,20},{4,12},{1,5},{9... | collective-permute-start | bytes 442376 | tf_op jit(solution)/shard_map/ppermute | solution.py:293
  14.3 3.3 %collective-permute-start.3 = (f32[288,128]{1,0:T(8,128)S(1)}, f32[288,128]{1,0:T(8,128)S(1)}, u32[]{:S(2)}, u32[]{:S(2)}) collective-permute-start(f32[288,128]{1,0:T(8,128)S(1)} %get-tuple-element.80), channel_id=1, source_target_pairs={{0,8},{8,16},{16,24},{24,28},{28,20},{20,12},{12,4},{4,0},{1,9},{9... | collective-permute-start | bytes 442376 | tf_op jit(solution)/shard_map/ppermute | solution.py:293
  17.7 1.6 collective-permute-start.2
  19.9 2.4 %collective-permute-done.4 = f32[288,128]{1,0:T(8,128)S(1)} collective-permute-done((f32[288,128]{1,0:T(8,128)S(1)}, f32[288,128]{1,0:T(8,128)S(1)}, u32[]{:S(2)}, u32[]{:S(2)}) %collective-permute-start.4) | collective-permute-done | bytes 147488 | tf_op jit(solution)/shard_map/ppermute | solution.py:293
  27.6 1.4 collective-permute-done.8
  34.4 1.4 collective-permute-done.12
  36.7 2.8 %collective-permute-done.9 = f32[288,128]{1,0:T(8,128)S(1)} collective-permute-done((f32[288,128]{1,0:T(8,128)S(1)}, f32[288,128]{1,0:T(8,128)S(1)}, u32[]{:S(2)}, u32[]{:S(2)}) %collective-permute-start.9) | collective-permute-done | bytes 147488 | tf_op jit(solution)/shard_map/ppermute | solution.py:293
  39.6 5.1 %collective-permute-done.13 = f32[288,128]{1,0:T(8,128)S(1)} collective-permute-done((f32[288,128]{1,0:T(8,128)S(1)}, f32[288,128]{1,0:T(8,128)S(1)}, u32[]{:S(2)}, u32[]{:S(2)}) %collective-permute-start.13) | collective-permute-done | bytes 147488 | tf_op jit(solution)/shard_map/ppermute | solution.py:293
  44.9 1.4 copy-done
  46.3 20.6 %panel_product.1 = (f32[2304,4608]{1,0:T(8,128)S(1)}, f32[2,576,128]{2,1,0:T(8,128)}, f32[2,576,128]{2,1,0:T(8,128)}, f32[128,128]{1,0:T(8,128)}) custom-call(s32[2]{0:T(128)} %pad_add_fusion.here_ref, f32[2304,4608]{1,0:T(8,128)} %h_ref.1, f32[2,2304,128]{2,1,0:T(8,128)} %bitcast.117), custom_call_target="tpu_custom_call" | custom-call | flops 10871635968 | bytes 42467328 | tf_op jit(solution)/shard_map/panel_product/pallas_call | solution.py:131
  67.0 1.4 collective-permute-start.20
  68.4 8.0 %collective-permute-done.20 = f32[576,128]{1,0:T(8,128)S(1)} collective-permute-done((f32[576,128]{1,0:T(8,128)S(1)}, f32[576,128]{1,0:T(8,128)S(1)}, u32[]{:S(2)}, u32[]{:S(2)}) %collective-permute-start.20) | collective-permute-done | bytes 294944 | tf_op jit(solution)/shard_map/ppermute | solution.py:286
  80.4 1.4 collective-permute-start.41
  82.5 3.7 %collective-permute-done.41 = f32[128,128]{1,0:T(8,128)S(1)} collective-permute-done((f32[128,128]{1,0:T(8,128)S(1)}, f32[128,128]{1,0:T(8,128)S(1)}, u32[]{:S(2)}, u32[]{:S(2)}) %collective-permute-start.41) | collective-permute-done | bytes 65568 | tf_op jit(solution)/shard_map/ppermute | solution.py:328
  88.1 3.8 %collective-permute-start.17 = (f32[576,128]{1,0:T(8,128)S(1)}, f32[576,128]{1,0:T(8,128)S(1)}, u32[]{:S(2)}, u32[]{:S(2)}) collective-permute-start(f32[576,128]{1,0:T(8,128)S(1)} %get-tuple-element.62), channel_id=1, source_target_pairs={{0,8},{1,12},{2,0},{3,4},{4,9},{5,13},{6,1},{7,5},{8,10},{9,14},{1... | collective-permute-start | bytes 884744 | tf_op jit(solution)/shard_map/ppermute | solution.py:279
  96.3 2.9 %collective-permute-done.17 = f32[576,128]{1,0:T(8,128)S(1)} collective-permute-done((f32[576,128]{1,0:T(8,128)S(1)}, f32[576,128]{1,0:T(8,128)S(1)}, u32[]{:S(2)}, u32[]{:S(2)}) %collective-permute-start.17) | collective-permute-done | bytes 294944 | tf_op jit(solution)/shard_map/ppermute | solution.py:279
  99.5 2.5 %collective-permute-start.18 = (f32[288,128]{1,0:T(8,128)S(1)}, f32[288,128]{1,0:T(8,128)S(1)}, u32[]{:S(2)}, u32[]{:S(2)}) collective-permute-start(f32[288,128]{1,0:T(8,128)S(1)} %get-tuple-element.79), channel_id=1, source_target_pairs={{0,8},{8,16},{16,24},{24,28},{28,20},{20,12},{12,4},{4,0},{1,9},{9... | collective-permute-start | bytes 442376 | tf_op jit(solution)/shard_map/ppermute | solution.py:293
  104.3 3.1 %collective-permute-done.45 = f32[128,128]{1,0:T(8,128)S(1)} collective-permute-done((f32[128,128]{1,0:T(8,128)S(1)}, f32[128,128]{1,0:T(8,128)S(1)}, u32[]{:S(2)}, u32[]{:S(2)}) %collective-permute-start.45) | collective-permute-done | bytes 65568 | tf_op jit(solution)/shard_map/ppermute | solution.py:334
  107.4 2.1 %collective-permute-start.28 = (f32[288,128]{1,0:T(8,128)S(1)}, f32[288,128]{1,0:T(8,128)S(1)}, u32[]{:S(2)}, u32[]{:S(2)}) collective-permute-start(f32[288,128]{1,0:T(8,128)S(1)} %get-tuple-element.79), channel_id=1, source_target_pairs={{0,4},{8,0},{16,8},{24,16},{28,24},{20,28},{12,20},{4,12},{1,5},{9... | collective-permute-start | bytes 442376 | tf_op jit(solution)/shard_map/ppermute | solution.py:293
  109.5 1.3 collective-permute-start.22
  113.8 1.6 collective-permute-start.31
  116.0 2.1 %collective-permute-done.22 = f32[576,128]{1,0:T(8,128)S(1)} collective-permute-done((f32[576,128]{1,0:T(8,128)S(1)}, f32[576,128]{1,0:T(8,128)S(1)}, u32[]{:S(2)}, u32[]{:S(2)}) %collective-permute-start.22) | collective-permute-done | bytes 294944 | tf_op jit(solution)/shard_map/ppermute | solution.py:286
  118.1 1.8 %collective-permute-start.26 = (f32[576,128]{1,0:T(8,128)S(1)}, f32[576,128]{1,0:T(8,128)S(1)}, u32[]{:S(2)}, u32[]{:S(2)}) collective-permute-start(f32[576,128]{1,0:T(8,128)S(1)} %fusion.25), channel_id=1, source_target_pairs={{0,2},{1,3},{2,0},{3,1},{4,6},{5,7},{6,4},{7,5},{8,10},{9,11},{10,... | collective-permute-start | bytes 884744 | tf_op jit(solution)/shard_map/ppermute | solution.py:286
  120.9 2.0 %collective-permute-start.47 = (f32[128,128]{1,0:T(8,128)S(1)}, f32[128,128]{1,0:T(8,128)S(1)}, u32[]{:S(2)}, u32[]{:S(2)}) collective-permute-start(f32[128,128]{1,0:T(8,128)S(1)} %add.277), channel_id=1, source_target_pairs={{0,16},{4,20},{8,24},{12,28},{16,0},{20,4},{24,8},{28,12},{1,17},{... | collective-permute-start | bytes 196616 | tf_op jit(solution)/shard_map/ppermute | solution.py:334
  123.6 1.3 collective-permute-start.35
  125.7 1.7 %collective-permute-done.47 = f32[128,128]{1,0:T(8,128)S(1)} collective-permute-done((f32[128,128]{1,0:T(8,128)S(1)}, f32[128,128]{1,0:T(8,128)S(1)}, u32[]{:S(2)}, u32[]{:S(2)}) %collective-permute-start.47) | collective-permute-done | bytes 65568 | tf_op jit(solution)/shard_map/ppermute | solution.py:334
  129.2 3.4 %collective-permute-done.24 = f32[288,128]{1,0:T(8,128)S(1)} collective-permute-done((f32[288,128]{1,0:T(8,128)S(1)}, f32[288,128]{1,0:T(8,128)S(1)}, u32[]{:S(2)}, u32[]{:S(2)}) %collective-permute-start.24) | collective-permute-done | bytes 147488 | tf_op jit(solution)/shard_map/ppermute | solution.py:293
  133.4 1.4 collective-permute-start.38
  135.0 4.1 %collective-permute-done.37 = f32[288,128]{1,0:T(8,128)S(1)} collective-permute-done((f32[288,128]{1,0:T(8,128)S(1)}, f32[288,128]{1,0:T(8,128)S(1)}, u32[]{:S(2)}, u32[]{:S(2)}) %collective-permute-start.37) | collective-permute-done | bytes 147488 | tf_op jit(solution)/shard_map/ppermute | solution.py:293
  139.5 1.3 copy-done.1
  141.2 26.2 %rank_update.1 = f32[2304,4608]{1,0:T(8,128)} custom-call(f32[2304,4608]{1,0:T(8,128)S(1)} %get-tuple-element.48.refs_0_, f32[2304,128]{1,0:T(8,128)} %bitcast.121, f32[2304,128]{1,0:T(8,128)} %bitcast.120, f32[2,2304,128]{2,1,0:T(8,128)} %bitcast.118, f32[2,2304,128]{2,1,0:T(8,128)} %bitcast.119, f32[256,128]{1,0:T(8,128)} %pad_maximum_fusion.refs_5_), custom_call_target="tpu_custom_call" | custom-call | flops 16307453952 | bytes 84934656 | tf_op jit(solution)/shard_map/rank_update/pallas_call | solution.py:223
  (158 shorter events, 36.6 us)
Async XLA Ops:
  2.7 19.6 %collective-permute-start.4 = (f32[288,128]{1,0:T(8,128)S(1)}, f32[288,128]{1,0:T(8,128)S(1)}, u32[]{:S(2)}, u32[]{:S(2)}) collective-permute-start(f32[288,128]{1,0:T(8,128)S(1)} %get-tuple-element.80), channel_id=1, source_target_pairs={{0,4},{8,0},{16,8},{24,16},{28,24},{20,28},{12,20},{4,12},{1,5},{9... | collective-permute-start | bytes 442376 | tf_op jit(solution)/shard_map/ppermute | solution.py:293
  14.3 8.9 %collective-permute-start.3 = (f32[288,128]{1,0:T(8,128)S(1)}, f32[288,128]{1,0:T(8,128)S(1)}, u32[]{:S(2)}, u32[]{:S(2)}) collective-permute-start(f32[288,128]{1,0:T(8,128)S(1)} %get-tuple-element.80), channel_id=1, source_target_pairs={{0,8},{8,16},{16,24},{24,28},{28,20},{20,12},{12,4},{4,0},{1,9},{9... | collective-permute-start | bytes 442376 | tf_op jit(solution)/shard_map/ppermute | solution.py:293
  17.7 7.8 %collective-permute-start.2 = (f32[288,128]{1,0:T(8,128)S(1)}, f32[288,128]{1,0:T(8,128)S(1)}, u32[]{:S(2)}, u32[]{:S(2)}) collective-permute-start(f32[288,128]{1,0:T(8,128)S(1)} %get-tuple-element.81), channel_id=1, source_target_pairs={{0,4},{8,0},{16,8},{24,16},{28,24},{20,28},{12,20},{4,12},{1,5},{9... | collective-permute-start | bytes 442376 | tf_op jit(solution)/shard_map/ppermute | solution.py:293
  19.2 7.2 %collective-permute-start.1 = (f32[288,128]{1,0:T(8,128)S(1)}, f32[288,128]{1,0:T(8,128)S(1)}, u32[]{:S(2)}, u32[]{:S(2)}) collective-permute-start(f32[288,128]{1,0:T(8,128)S(1)} %get-tuple-element.81), channel_id=1, source_target_pairs={{0,8},{8,16},{16,24},{24,28},{28,20},{20,12},{12,4},{4,0},{1,9},{9... | collective-permute-start | bytes 442376 | tf_op jit(solution)/shard_map/ppermute | solution.py:293
  22.3 6.7 %collective-permute-start.8 = (f32[288,128]{1,0:T(8,128)S(1)}, f32[288,128]{1,0:T(8,128)S(1)}, u32[]{:S(2)}, u32[]{:S(2)}) collective-permute-start(f32[288,128]{1,0:T(8,128)S(1)} %collective-permute-done.4), channel_id=1, source_target_pairs={{0,4},{8,0},{16,8},{24,16},{28,24},{20,28},{12,20},{4,12},{1,5},{9... | collective-permute-start | bytes 442376 | tf_op jit(solution)/shard_map/ppermute | solution.py:293
  23.3 7.0 %collective-permute-start.7 = (f32[288,128]{1,0:T(8,128)S(1)}, f32[288,128]{1,0:T(8,128)S(1)}, u32[]{:S(2)}, u32[]{:S(2)}) collective-permute-start(f32[288,128]{1,0:T(8,128)S(1)} %collective-permute-done.3), channel_id=1, source_target_pairs={{0,8},{8,16},{16,24},{24,28},{28,20},{20,12},{12,4},{4,0},{1,9},{9... | collective-permute-start | bytes 442376 | tf_op jit(solution)/shard_map/ppermute | solution.py:293
  25.5 6.7 %collective-permute-start.6 = (f32[288,128]{1,0:T(8,128)S(1)}, f32[288,128]{1,0:T(8,128)S(1)}, u32[]{:S(2)}, u32[]{:S(2)}) collective-permute-start(f32[288,128]{1,0:T(8,128)S(1)} %collective-permute-done.2), channel_id=1, source_target_pairs={{0,4},{8,0},{16,8},{24,16},{28,24},{20,28},{12,20},{4,12},{1,5},{9... | collective-permute-start | bytes 442376 | tf_op jit(solution)/shard_map/ppermute | solution.py:293
  26.4 7.0 %collective-permute-start.5 = (f32[288,128]{1,0:T(8,128)S(1)}, f32[288,128]{1,0:T(8,128)S(1)}, u32[]{:S(2)}, u32[]{:S(2)}) collective-permute-start(f32[288,128]{1,0:T(8,128)S(1)} %collective-permute-done.1), channel_id=1, source_target_pairs={{0,8},{8,16},{16,24},{24,28},{28,20},{20,12},{12,4},{4,0},{1,9},{9... | collective-permute-start | bytes 442376 | tf_op jit(solution)/shard_map/ppermute | solution.py:293
  29.0 6.7 %collective-permute-start.12 = (f32[288,128]{1,0:T(8,128)S(1)}, f32[288,128]{1,0:T(8,128)S(1)}, u32[]{:S(2)}, u32[]{:S(2)}) collective-permute-start(f32[288,128]{1,0:T(8,128)S(1)} %collective-permute-done.8), channel_id=1, source_target_pairs={{0,4},{8,0},{16,8},{24,16},{28,24},{20,28},{12,20},{4,12},{1,5},{9... | collective-permute-start | bytes 442376 | tf_op jit(solution)/shard_map/ppermute | solution.py:293
  30.3 9.3 %collective-permute-start.11 = (f32[288,128]{1,0:T(8,128)S(1)}, f32[288,128]{1,0:T(8,128)S(1)}, u32[]{:S(2)}, u32[]{:S(2)}) collective-permute-start(f32[288,128]{1,0:T(8,128)S(1)} %collective-permute-done.7), channel_id=1, source_target_pairs={{0,8},{8,16},{16,24},{24,28},{28,20},{20,12},{12,4},{4,0},{1,9},{9... | collective-permute-start | bytes 442376 | tf_op jit(solution)/shard_map/ppermute | solution.py:293
  32.2 7.4 %collective-permute-start.10 = (f32[288,128]{1,0:T(8,128)S(1)}, f32[288,128]{1,0:T(8,128)S(1)}, u32[]{:S(2)}, u32[]{:S(2)}) collective-permute-start(f32[288,128]{1,0:T(8,128)S(1)} %collective-permute-done.6), channel_id=1, source_target_pairs={{0,4},{8,0},{16,8},{24,16},{28,24},{20,28},{12,20},{4,12},{1,5},{9... | collective-permute-start | bytes 442376 | tf_op jit(solution)/shard_map/ppermute | solution.py:293
  35.7 9.1 %collective-permute-start.14 = (f32[288,128]{1,0:T(8,128)S(1)}, f32[288,128]{1,0:T(8,128)S(1)}, u32[]{:S(2)}, u32[]{:S(2)}) collective-permute-start(f32[288,128]{1,0:T(8,128)S(1)} %collective-permute-done.12), channel_id=1, source_target_pairs={{0,4},{8,0},{16,8},{24,16},{28,24},{20,28},{12,20},{4,12},{1,5},{9... | collective-permute-start | bytes 442376 | tf_op jit(solution)/shard_map/ppermute | solution.py:293
  66.9 9.5 %collective-permute-start.15 = (f32[2,576,128]{2,1,0:T(8,128)}, f32[2,576,128]{2,1,0:T(8,128)S(1)}, u32[]{:S(2)}, u32[]{:S(2)}) collective-permute-start(f32[2,576,128]{2,1,0:T(8,128)} %get-tuple-element.52), channel_id=1, source_target_pairs={{0,1},{1,0},{2,3},{3,2},{4,5},{5,4},{6,7},{7,6},{8,9},{9,8},{10,11... | collective-permute-start | bytes 1769480 | tf_op jit(solution)/shard_map/ppermute | solution.py:282
  67.0 9.4 %collective-permute-start.20 = (f32[576,128]{1,0:T(8,128)S(1)}, f32[576,128]{1,0:T(8,128)S(1)}, u32[]{:S(2)}, u32[]{:S(2)}) collective-permute-start(f32[576,128]{1,0:T(8,128)S(1)} %select_select_fusion), channel_id=1, source_target_pairs={{0,2},{1,3},{2,0},{3,1},{4,6},{5,7},{6,4},{7,5},{8,10},{9,11},{10,... | collective-permute-start | bytes 884744 | tf_op jit(solution)/shard_map/ppermute | solution.py:286
  78.9 16.4 %collective-permute-start.44 = (f32[128,128]{1,0:T(8,128)S(1)}, f32[128,128]{1,0:T(8,128)S(1)}, u32[]{:S(2)}, u32[]{:S(2)}) collective-permute-start(f32[128,128]{1,0:T(8,128)S(1)} %convolution_add_fusion.1), channel_id=1, source_target_pairs={{0,3},{1,2},{2,1},{3,0},{4,7},{5,6},{6,5},{7,4},{8,11},{9,10},{10,... | collective-permute-start | bytes 196616 | tf_op jit(solution)/shard_map/ppermute | solution.py:328
  79.5 16.7 %collective-permute-start.43 = (f32[128,128]{1,0:T(8,128)S(1)}, f32[128,128]{1,0:T(8,128)S(1)}, u32[]{:S(2)}, u32[]{:S(2)}) collective-permute-start(f32[128,128]{1,0:T(8,128)S(1)} %convolution_add_fusion.1), channel_id=1, source_target_pairs={{0,2},{1,3},{2,0},{3,1},{4,6},{5,7},{6,4},{7,5},{8,10},{9,11},{10,... | collective-permute-start | bytes 196616 | tf_op jit(solution)/shard_map/ppermute | solution.py:328
  86.2 10.1 %collective-permute-start.42 = (f32[128,128]{1,0:T(8,128)S(1)}, f32[128,128]{1,0:T(8,128)S(1)}, u32[]{:S(2)}, u32[]{:S(2)}) collective-permute-start(f32[128,128]{1,0:T(8,128)S(1)} %convolution_add_fusion.1), channel_id=1, source_target_pairs={{0,1},{1,0},{2,3},{3,2},{4,5},{5,4},{6,7},{7,6},{8,9},{9,8},{10,11... | collective-permute-start | bytes 196616 | tf_op jit(solution)/shard_map/ppermute | solution.py:328
  87.4 8.9 %collective-permute-start.16 = (f32[576,128]{1,0:T(8,128)S(1)}, f32[576,128]{1,0:T(8,128)S(1)}, u32[]{:S(2)}, u32[]{:S(2)}) collective-permute-start(f32[576,128]{1,0:T(8,128)S(1)} %get-tuple-element.77), channel_id=1, source_target_pairs={{0,0},{1,4},{2,8},{3,12},{4,1},{5,5},{6,9},{7,13},{8,2},{9,6},{10,... | collective-permute-start | bytes 884744 | tf_op jit(solution)/shard_map/ppermute | solution.py:279
  88.1 11.1 %collective-permute-start.17 = (f32[576,128]{1,0:T(8,128)S(1)}, f32[576,128]{1,0:T(8,128)S(1)}, u32[]{:S(2)}, u32[]{:S(2)}) collective-permute-start(f32[576,128]{1,0:T(8,128)S(1)} %get-tuple-element.62), channel_id=1, source_target_pairs={{0,8},{1,12},{2,0},{3,4},{4,9},{5,13},{6,1},{7,5},{8,10},{9,14},{1... | collective-permute-start | bytes 884744 | tf_op jit(solution)/shard_map/ppermute | solution.py:279
  95.4 15.4 %collective-permute-start.19 = (f32[576,128]{1,0:T(8,128)S(1)}, f32[576,128]{1,0:T(8,128)S(1)}, u32[]{:S(2)}, u32[]{:S(2)}) collective-permute-start(f32[576,128]{1,0:T(8,128)S(1)} %select_select_fusion), channel_id=1, source_target_pairs={{0,1},{1,0},{2,3},{3,2},{4,5},{5,4},{6,7},{7,6},{8,9},{9,8},{10,11... | collective-permute-start | bytes 884744 | tf_op jit(solution)/shard_map/ppermute | solution.py:282
  96.2 13.3 %collective-permute-start.21 = (f32[576,128]{1,0:T(8,128)S(1)}, f32[576,128]{1,0:T(8,128)S(1)}, u32[]{:S(2)}, u32[]{:S(2)}) collective-permute-start(f32[576,128]{1,0:T(8,128)S(1)} %collective-permute-done.20), channel_id=1, source_target_pairs={{0,1},{1,0},{2,3},{3,2},{4,5},{5,4},{6,7},{7,6},{8,9},{9,8},{10,11... | collective-permute-start | bytes 884744 | tf_op jit(solution)/shard_map/ppermute | solution.py:282
  99.5 7.9 %collective-permute-start.18 = (f32[288,128]{1,0:T(8,128)S(1)}, f32[288,128]{1,0:T(8,128)S(1)}, u32[]{:S(2)}, u32[]{:S(2)}) collective-permute-start(f32[288,128]{1,0:T(8,128)S(1)} %get-tuple-element.79), channel_id=1, source_target_pairs={{0,8},{8,16},{16,24},{24,28},{28,20},{20,12},{12,4},{4,0},{1,9},{9... | collective-permute-start | bytes 442376 | tf_op jit(solution)/shard_map/ppermute | solution.py:293
  103.1 8.1 %collective-permute-start.30 = (f32[288,128]{1,0:T(8,128)S(1)}, f32[288,128]{1,0:T(8,128)S(1)}, u32[]{:S(2)}, u32[]{:S(2)}) collective-permute-start(f32[288,128]{1,0:T(8,128)S(1)} %get-tuple-element.78), channel_id=1, source_target_pairs={{0,4},{8,0},{16,8},{24,16},{28,24},{20,28},{12,20},{4,12},{1,5},{9... | collective-permute-start | bytes 442376 | tf_op jit(solution)/shard_map/ppermute | solution.py:293
  109.5 8.6 %collective-permute-start.22 = (f32[576,128]{1,0:T(8,128)S(1)}, f32[576,128]{1,0:T(8,128)S(1)}, u32[]{:S(2)}, u32[]{:S(2)}) collective-permute-start(f32[576,128]{1,0:T(8,128)S(1)} %get-tuple-element.62), channel_id=1, source_target_pairs={{0,2},{1,3},{2,0},{3,1},{4,6},{5,7},{6,4},{7,5},{8,10},{9,11},{10,... | collective-permute-start | bytes 884744 | tf_op jit(solution)/shard_map/ppermute | solution.py:286
  111.1 11.7 %collective-permute-start.33 = (f32[288,128]{1,0:T(8,128)S(1)}, f32[288,128]{1,0:T(8,128)S(1)}, u32[]{:S(2)}, u32[]{:S(2)}) collective-permute-start(f32[288,128]{1,0:T(8,128)S(1)} %collective-permute-done.30), channel_id=1, source_target_pairs={{0,4},{8,0},{16,8},{24,16},{28,24},{20,28},{12,20},{4,12},{1,5},{9... | collective-permute-start | bytes 442376 | tf_op jit(solution)/shard_map/ppermute | solution.py:293
  112.5 11.1 %collective-permute-start.32 = (f32[288,128]{1,0:T(8,128)S(1)}, f32[288,128]{1,0:T(8,128)S(1)}, u32[]{:S(2)}, u32[]{:S(2)}) collective-permute-start(f32[288,128]{1,0:T(8,128)S(1)} %collective-permute-done.29), channel_id=1, source_target_pairs={{0,8},{8,16},{16,24},{24,28},{28,20},{20,12},{12,4},{4,0},{1,9},{9... | collective-permute-start | bytes 442376 | tf_op jit(solution)/shard_map/ppermute | solution.py:293
  113.8 11.2 %collective-permute-start.31 = (f32[288,128]{1,0:T(8,128)S(1)}, f32[288,128]{1,0:T(8,128)S(1)}, u32[]{:S(2)}, u32[]{:S(2)}) collective-permute-start(f32[288,128]{1,0:T(8,128)S(1)} %collective-permute-done.28), channel_id=1, source_target_pairs={{0,4},{8,0},{16,8},{24,16},{28,24},{20,28},{12,20},{4,12},{1,5},{9... | collective-permute-start | bytes 442376 | tf_op jit(solution)/shard_map/ppermute | solution.py:293
  118.1 16.8 %collective-permute-start.26 = (f32[576,128]{1,0:T(8,128)S(1)}, f32[576,128]{1,0:T(8,128)S(1)}, u32[]{:S(2)}, u32[]{:S(2)}) collective-permute-start(f32[576,128]{1,0:T(8,128)S(1)} %fusion.25), channel_id=1, source_target_pairs={{0,2},{1,3},{2,0},{3,1},{4,6},{5,7},{6,4},{7,5},{8,10},{9,11},{10,... | collective-permute-start | bytes 884744 | tf_op jit(solution)/shard_map/ppermute | solution.py:286
  122.9 9.9 %collective-permute-start.36 = (f32[288,128]{1,0:T(8,128)S(1)}, f32[288,128]{1,0:T(8,128)S(1)}, u32[]{:S(2)}, u32[]{:S(2)}) collective-permute-start(f32[288,128]{1,0:T(8,128)S(1)} %collective-permute-done.33), channel_id=1, source_target_pairs={{0,4},{8,0},{16,8},{24,16},{28,24},{20,28},{12,20},{4,12},{1,5},{9... | collective-permute-start | bytes 442376 | tf_op jit(solution)/shard_map/ppermute | solution.py:293
  123.6 11.2 %collective-permute-start.35 = (f32[288,128]{1,0:T(8,128)S(1)}, f32[288,128]{1,0:T(8,128)S(1)}, u32[]{:S(2)}, u32[]{:S(2)}) collective-permute-start(f32[288,128]{1,0:T(8,128)S(1)} %collective-permute-done.32), channel_id=1, source_target_pairs={{0,8},{8,16},{16,24},{24,28},{28,20},{20,12},{12,4},{4,0},{1,9},{9... | collective-permute-start | bytes 442376 | tf_op jit(solution)/shard_map/ppermute | solution.py:293
  124.9 8.5 %collective-permute-start.34 = (f32[288,128]{1,0:T(8,128)S(1)}, f32[288,128]{1,0:T(8,128)S(1)}, u32[]{:S(2)}, u32[]{:S(2)}) collective-permute-start(f32[288,128]{1,0:T(8,128)S(1)} %collective-permute-done.31), channel_id=1, source_target_pairs={{0,4},{8,0},{16,8},{24,16},{28,24},{20,28},{12,20},{4,12},{1,5},{9... | collective-permute-start | bytes 442376 | tf_op jit(solution)/shard_map/ppermute | solution.py:293
  132.6 6.8 %collective-permute-start.25 = (f32[576,128]{1,0:T(8,128)S(1)}, f32[576,128]{1,0:T(8,128)S(1)}, u32[]{:S(2)}, u32[]{:S(2)}) collective-permute-start(f32[576,128]{1,0:T(8,128)S(1)} %fusion.25), channel_id=1, source_target_pairs={{0,1},{1,0},{2,3},{3,2},{4,5},{5,4},{6,7},{7,6},{8,9},{9,8},{10,11... | collective-permute-start | bytes 884744 | tf_op jit(solution)/shard_map/ppermute | solution.py:282
  (23 other events, 229.8 us)

commit v2 on v1

--- a/solution.py
+++ b/solution.py
@@ -269,12 +269,15 @@
         self.places, self.same_core, self.other, self.here = known
         return x
 
+    def turned(self, j):
+        return (self.pairs - 1 - j // 2) * 2 + j % 2
+
     def to_shard(self, x, shift):
         route = []
         for g in range(self.rows):
             for c in range(self.cols):
                 piece = (c // 2 + shift) % self.pairs * 2 + c % 2
-                target = g // self.cols * self.cols + piece
+                target = g // self.cols * self.cols + self.turned(piece)
                 route.append((g * self.cols + c, target * self.cols + g % self.cols))
         return lax.ppermute(x, BOTH, route)
 
@@ -299,7 +302,8 @@
         r = self.row
         here = jnp.where(r % 2 == 0, r // 2, n - 1 - r // 2)
         there = (here - shift) % n
-        return jnp.where(there < n // 2, 2 * there, 2 * (n - there) - 1)
+        row = jnp.where(there < n // 2, 2 * there, 2 * (n - there) - 1)
+        return row // self.cols * self.cols + self.turned(row % self.cols)
 
     def gather_ring(self, shard, asides=()):
         n = self.rows
@@ -378,7 +382,8 @@
     groups = place.rows // place.cols
     position = place.col * piece_rows + jnp.arange(piece_rows, dtype=jnp.int32)
     global_rows = (position // B * place.rows + place.row) * B + position % B
-    piece = place.before(shape_panel(panel, global_rows, B))
+    piece = shape_panel(panel, global_rows, B)
+    hamiltonian = place.before(hamiltonian)
 
     sums = {}
 

time: 168 us -> 166 us (0.988)
  starting transfers between devices: 57.9 us -> 46.9 us
  waiting for transfers between devices: 48.3 us -> 57.5 us
    ppermute x28, starting transfers between devices: 40.7 us -> 26.1 us  [ring(): lax.ppermute(x, 'row', [(order[i], order[(i + shift) % n]) for i in range...]
    ppermute x3, waiting for transfers between devices: 2.93 us -> 8.58 us  [to_shard(): return lax.ppermute(x, BOTH, route)]
    ppermute x3, waiting for transfers between devices: 5.02 us -> 8.52 us  [other_bit(): return lax.ppermute(x, 'row', [(r, r ^ bit) for r in range(n)])]
    ppermute x5, starting transfers between devices: 1.03 us -> 4.31 us  [other_core(): return lax.ppermute(x, 'col', [(c, c ^ 1) for c in range(self.cols)])]
    ppermute x3, starting transfers between devices: 4.53 us -> 6.75 us  [along_pairs(): lax.ppermute(x, 'col', [(c, (c // 2 + shift) % n * 2 + c % 2) for c in ra...]
  transfers between devices with their start and end apart: 48 -> 48, of which waited for: 22 -> 20; matrix products, arithmetic and copies ran while one was open for 4% -> 4% of each run, Pallas kernels for 0% -> 0%
where the time goes in v2:
time: 166 us
  waiting for transfers between devices  57.5 us (35%)
  starting transfers between devices  46.9 us (28%)
  Pallas kernels  46.8 us (28%)
  matrix products  5.31 us (3%)
  local copies, waits for them, and re-layouts  4.32 us (3%)
  other arithmetic  3.92 us (2%)
    ppermute x28, waiting for transfers between devices, ring(): lax.ppermute(x, 'row', [(order[i], order[(i + shift) % n]) for i in range...  26.4 us
    pallas_call x1, Pallas kernels, update(): pl.pallas_call(functools.partial(update_kernel, groups, width, per_step,...  26.2 us
    ppermute x28, starting transfers between devices, ring(): lax.ppermute(x, 'row', [(order[i], order[(i + shift) % n]) for i in range...  26.1 us
    pallas_call x1, Pallas kernels, product(): pl.pallas_call(functools.partial(product_kernel, groups, width, per_step,...  20.6 us
    ppermute x3, waiting for transfers between devices, along_pairs(): lax.ppermute(x, 'col', [(c, (c // 2 + shift) % n * 2 + c % 2) for c in ra...  9.38 us
    ppermute x3, waiting for transfers between devices, to_shard(): return lax.ppermute(x, BOTH, route)  8.58 us
    ppermute x3, waiting for transfers between devices, other_bit(): return lax.ppermute(x, 'row', [(r, r ^ bit) for r in range(n)])  8.52 us
    ppermute x3, starting transfers between devices, along_pairs(): lax.ppermute(x, 'col', [(c, (c // 2 + shift) % n * 2 + c % 2) for c in ra...  6.75 us
  transfers between devices with their start and end apart: 48, of which 20 were waited for; matrix products, arithmetic and copies ran while one was open for 4% of the time, Pallas kernels for 0%

profile of v2, /device:TPU:0, one launch (start us, length us, event | category | flops | bytes accessed | tf_op | source)
XLA Modules:
  0.0 165.6 jit_solution(8104476303185581299)
XLA Ops:
  0.1 1.3 select_select_fusion
  1.3 3.1 %collective-permute-start = (f32[576,128]{1,0:T(8,128)S(1)}, f32[576,128]{1,0:T(8,128)S(1)}, u32[]{:S(2)}, u32[]{:S(2)}) collective-permute-start(f32[576,128]{1,0:T(8,128)S(1)} %select_select_fusion), channel_id=1, source_target_pairs={{0,8},{1,12},{2,0},{3,4},{4,9},{5,13},{6,1},{7,5},{8,10},{9,14},{1... | collective-permute-start | bytes 884744 | tf_op jit(solution)/shard_map/ppermute | solution.py:282
  5.0 7.2 %collective-permute-done = f32[576,128]{1,0:T(8,128)S(1)} collective-permute-done((f32[576,128]{1,0:T(8,128)S(1)}, f32[576,128]{1,0:T(8,128)S(1)}, u32[]{:S(2)}, u32[]{:S(2)}) %collective-permute-start) | collective-permute-done | bytes 294944 | tf_op jit(solution)/shard_map/ppermute | solution.py:282
  12.3 1.5 collective-permute-start.4
  14.3 1.6 collective-permute-start.2
  16.5 2.5 %collective-permute-done.4 = f32[288,128]{1,0:T(8,128)S(1)} collective-permute-done((f32[288,128]{1,0:T(8,128)S(1)}, f32[288,128]{1,0:T(8,128)S(1)}, u32[]{:S(2)}, u32[]{:S(2)}) %collective-permute-start.4) | collective-permute-done | bytes 147488 | tf_op jit(solution)/shard_map/ppermute | solution.py:296
  24.3 1.4 collective-permute-done.8
  31.0 1.4 collective-permute-done.12
  33.5 3.2 %collective-permute-done.9 = f32[288,128]{1,0:T(8,128)S(1)} collective-permute-done((f32[288,128]{1,0:T(8,128)S(1)}, f32[288,128]{1,0:T(8,128)S(1)}, u32[]{:S(2)}, u32[]{:S(2)}) %collective-permute-start.9) | collective-permute-done | bytes 147488 | tf_op jit(solution)/shard_map/ppermute | solution.py:296
  36.9 5.0 %collective-permute-done.13 = f32[288,128]{1,0:T(8,128)S(1)} collective-permute-done((f32[288,128]{1,0:T(8,128)S(1)}, f32[288,128]{1,0:T(8,128)S(1)}, u32[]{:S(2)}, u32[]{:S(2)}) %collective-permute-start.13) | collective-permute-done | bytes 147488 | tf_op jit(solution)/shard_map/ppermute | solution.py:296
  42.0 1.4 copy-done
  43.4 20.6 %panel_product.1 = (f32[2304,4608]{1,0:T(8,128)S(1)}, f32[2,576,128]{2,1,0:T(8,128)}, f32[2,576,128]{2,1,0:T(8,128)}, f32[128,128]{1,0:T(8,128)}) custom-call(s32[2]{0:T(128)} %pad_add_fusion.here_ref, f32[2304,4608]{1,0:T(8,128)} %h_ref, f32[2,2304,128]{2,1,0:T(8,128)} %bitcast.117), custom_call_target="tpu_custom_call" | custom-call | flops 10871635968 | bytes 42467328 | tf_op jit(solution)/shard_map/panel_product/pallas_call | solution.py:131
  64.9 8.5 %collective-permute-done.20 = f32[576,128]{1,0:T(8,128)S(1)} collective-permute-done((f32[576,128]{1,0:T(8,128)S(1)}, f32[576,128]{1,0:T(8,128)S(1)}, u32[]{:S(2)}, u32[]{:S(2)}) %collective-permute-start.20) | collective-permute-done | bytes 294944 | tf_op jit(solution)/shard_map/ppermute | solution.py:289
  79.6 3.7 %collective-permute-done.41 = f32[128,128]{1,0:T(8,128)S(1)} collective-permute-done((f32[128,128]{1,0:T(8,128)S(1)}, f32[128,128]{1,0:T(8,128)S(1)}, u32[]{:S(2)}, u32[]{:S(2)}) %collective-permute-start.41) | collective-permute-done | bytes 65568 | tf_op jit(solution)/shard_map/ppermute | solution.py:332
  88.4 4.1 %collective-permute-start.19 = (f32[576,128]{1,0:T(8,128)S(1)}, f32[576,128]{1,0:T(8,128)S(1)}, u32[]{:S(2)}, u32[]{:S(2)}) collective-permute-start(f32[576,128]{1,0:T(8,128)S(1)} %select_select_fusion), channel_id=1, source_target_pairs={{0,1},{1,0},{2,3},{3,2},{4,5},{5,4},{6,7},{7,6},{8,9},{9,8},{10,11... | collective-permute-start | bytes 884744 | tf_op jit(solution)/shard_map/ppermute | solution.py:285
  92.6 1.4 collective-permute-done.16
  94.2 3.0 %collective-permute-start.18 = (f32[288,128]{1,0:T(8,128)S(1)}, f32[288,128]{1,0:T(8,128)S(1)}, u32[]{:S(2)}, u32[]{:S(2)}) collective-permute-start(f32[288,128]{1,0:T(8,128)S(1)} %get-tuple-element.79), channel_id=1, source_target_pairs={{0,8},{8,16},{16,24},{24,28},{28,20},{20,12},{12,4},{4,0},{1,9},{9... | collective-permute-start | bytes 442376 | tf_op jit(solution)/shard_map/ppermute | solution.py:296
  99.5 3.5 %collective-permute-done.45 = f32[128,128]{1,0:T(8,128)S(1)} collective-permute-done((f32[128,128]{1,0:T(8,128)S(1)}, f32[128,128]{1,0:T(8,128)S(1)}, u32[]{:S(2)}, u32[]{:S(2)}) %collective-permute-start.45) | collective-permute-done | bytes 65568 | tf_op jit(solution)/shard_map/ppermute | solution.py:338
  103.1 2.1 %collective-permute-start.28 = (f32[288,128]{1,0:T(8,128)S(1)}, f32[288,128]{1,0:T(8,128)S(1)}, u32[]{:S(2)}, u32[]{:S(2)}) collective-permute-start(f32[288,128]{1,0:T(8,128)S(1)} %get-tuple-element.79), channel_id=1, source_target_pairs={{0,4},{8,0},{16,8},{24,16},{28,24},{20,28},{12,20},{4,12},{1,5},{9... | collective-permute-start | bytes 442376 | tf_op jit(solution)/shard_map/ppermute | solution.py:296
  105.1 4.1 %collective-permute-start.22 = (f32[576,128]{1,0:T(8,128)S(1)}, f32[576,128]{1,0:T(8,128)S(1)}, u32[]{:S(2)}, u32[]{:S(2)}) collective-permute-start(f32[576,128]{1,0:T(8,128)S(1)} %get-tuple-element.62), channel_id=1, source_target_pairs={{0,2},{1,3},{2,0},{3,1},{4,6},{5,7},{6,4},{7,5},{8,10},{9,11},{10,... | collective-permute-start | bytes 884744 | tf_op jit(solution)/shard_map/ppermute | solution.py:289
  109.5 2.0 %collective-permute-start.32 = (f32[288,128]{1,0:T(8,128)S(1)}, f32[288,128]{1,0:T(8,128)S(1)}, u32[]{:S(2)}, u32[]{:S(2)}) collective-permute-start(f32[288,128]{1,0:T(8,128)S(1)} %collective-permute-done.29), channel_id=1, source_target_pairs={{0,8},{8,16},{16,24},{24,28},{28,20},{20,12},{12,4},{4,0},{1,9},{9... | collective-permute-start | bytes 442376 | tf_op jit(solution)/shard_map/ppermute | solution.py:296
  111.8 2.3 %collective-permute-done.46 = f32[128,128]{1,0:T(8,128)S(1)} collective-permute-done((f32[128,128]{1,0:T(8,128)S(1)}, f32[128,128]{1,0:T(8,128)S(1)}, u32[]{:S(2)}, u32[]{:S(2)}) %collective-permute-start.46) | collective-permute-done | bytes 65568 | tf_op jit(solution)/shard_map/ppermute | solution.py:338
  115.1 1.8 %collective-permute-start.26 = (f32[576,128]{1,0:T(8,128)S(1)}, f32[576,128]{1,0:T(8,128)S(1)}, u32[]{:S(2)}, u32[]{:S(2)}) collective-permute-start(f32[576,128]{1,0:T(8,128)S(1)} %fusion.25), channel_id=1, source_target_pairs={{0,2},{1,3},{2,0},{3,1},{4,6},{5,7},{6,4},{7,5},{8,10},{9,11},{10,... | collective-permute-start | bytes 884744 | tf_op jit(solution)/shard_map/ppermute | solution.py:289
  116.9 2.4 %collective-permute-done.23 = f32[288,128]{1,0:T(8,128)S(1)} collective-permute-done((f32[288,128]{1,0:T(8,128)S(1)}, f32[288,128]{1,0:T(8,128)S(1)}, u32[]{:S(2)}, u32[]{:S(2)}) %collective-permute-start.23) | collective-permute-done | bytes 147488 | tf_op jit(solution)/shard_map/ppermute | solution.py:296
  119.3 1.4 collective-permute-start.47
  121.0 1.7 %collective-permute-start.35 = (f32[288,128]{1,0:T(8,128)S(1)}, f32[288,128]{1,0:T(8,128)S(1)}, u32[]{:S(2)}, u32[]{:S(2)}) collective-permute-start(f32[288,128]{1,0:T(8,128)S(1)} %collective-permute-done.32), channel_id=1, source_target_pairs={{0,8},{8,16},{16,24},{24,28},{28,20},{20,12},{12,4},{4,0},{1,9},{9... | collective-permute-start | bytes 442376 | tf_op jit(solution)/shard_map/ppermute | solution.py:296
  123.2 2.7 %collective-permute-done.47 = f32[128,128]{1,0:T(8,128)S(1)} collective-permute-done((f32[128,128]{1,0:T(8,128)S(1)}, f32[128,128]{1,0:T(8,128)S(1)}, u32[]{:S(2)}, u32[]{:S(2)}) %collective-permute-start.47) | collective-permute-done | bytes 65568 | tf_op jit(solution)/shard_map/ppermute | solution.py:338
  127.0 4.0 %collective-permute-done.24 = f32[288,128]{1,0:T(8,128)S(1)} collective-permute-done((f32[288,128]{1,0:T(8,128)S(1)}, f32[288,128]{1,0:T(8,128)S(1)}, u32[]{:S(2)}, u32[]{:S(2)}) %collective-permute-start.24) | collective-permute-done | bytes 147488 | tf_op jit(solution)/shard_map/ppermute | solution.py:296
  131.2 2.0 %collective-permute-start.38 = (f32[288,128]{1,0:T(8,128)S(1)}, f32[288,128]{1,0:T(8,128)S(1)}, u32[]{:S(2)}, u32[]{:S(2)}) collective-permute-start(f32[288,128]{1,0:T(8,128)S(1)} %collective-permute-done.36), channel_id=1, source_target_pairs={{0,4},{8,0},{16,8},{24,16},{28,24},{20,28},{12,20},{4,12},{1,5},{9... | collective-permute-start | bytes 442376 | tf_op jit(solution)/shard_map/ppermute | solution.py:296
  133.4 4.1 %collective-permute-done.37 = f32[288,128]{1,0:T(8,128)S(1)} collective-permute-done((f32[288,128]{1,0:T(8,128)S(1)}, f32[288,128]{1,0:T(8,128)S(1)}, u32[]{:S(2)}, u32[]{:S(2)}) %collective-permute-start.37) | collective-permute-done | bytes 147488 | tf_op jit(solution)/shard_map/ppermute | solution.py:296
  137.7 1.3 copy-done.1
  139.4 26.2 %rank_update.1 = f32[2304,4608]{1,0:T(8,128)} custom-call(f32[2304,4608]{1,0:T(8,128)S(1)} %get-tuple-element.48.refs_0_, f32[2304,128]{1,0:T(8,128)} %bitcast.121, f32[2304,128]{1,0:T(8,128)} %bitcast.120, f32[2,2304,128]{2,1,0:T(8,128)} %bitcast.118, f32[2,2304,128]{2,1,0:T(8,128)} %bitcast.119, f32[256,128]{1,0:T(8,128)} %pad_maximum_fusion.refs_5_), custom_call_target="tpu_custom_call" | custom-call | flops 16307453952 | bytes 84934656 | tf_op jit(solution)/shard_map/rank_update/pallas_call | solution.py:223
  (158 shorter events, 32.3 us)
Async XLA Ops:
  1.3 10.9 %collective-permute-start = (f32[576,128]{1,0:T(8,128)S(1)}, f32[576,128]{1,0:T(8,128)S(1)}, u32[]{:S(2)}, u32[]{:S(2)}) collective-permute-start(f32[576,128]{1,0:T(8,128)S(1)} %select_select_fusion), channel_id=1, source_target_pairs={{0,8},{1,12},{2,0},{3,4},{4,9},{5,13},{6,1},{7,5},{8,10},{9,14},{1... | collective-permute-start | bytes 884744 | tf_op jit(solution)/shard_map/ppermute | solution.py:282
  12.3 6.8 %collective-permute-start.4 = (f32[288,128]{1,0:T(8,128)S(1)}, f32[288,128]{1,0:T(8,128)S(1)}, u32[]{:S(2)}, u32[]{:S(2)}) collective-permute-start(f32[288,128]{1,0:T(8,128)S(1)} %get-tuple-element.80), channel_id=1, source_target_pairs={{0,4},{8,0},{16,8},{24,16},{28,24},{20,28},{12,20},{4,12},{1,5},{9... | collective-permute-start | bytes 442376 | tf_op jit(solution)/shard_map/ppermute | solution.py:296
  14.3 7.9 %collective-permute-start.2 = (f32[288,128]{1,0:T(8,128)S(1)}, f32[288,128]{1,0:T(8,128)S(1)}, u32[]{:S(2)}, u32[]{:S(2)}) collective-permute-start(f32[288,128]{1,0:T(8,128)S(1)} %get-tuple-element.81), channel_id=1, source_target_pairs={{0,4},{8,0},{16,8},{24,16},{28,24},{20,28},{12,20},{4,12},{1,5},{9... | collective-permute-start | bytes 442376 | tf_op jit(solution)/shard_map/ppermute | solution.py:296
  16.0 7.1 %collective-permute-start.1 = (f32[288,128]{1,0:T(8,128)S(1)}, f32[288,128]{1,0:T(8,128)S(1)}, u32[]{:S(2)}, u32[]{:S(2)}) collective-permute-start(f32[288,128]{1,0:T(8,128)S(1)} %get-tuple-element.81), channel_id=1, source_target_pairs={{0,8},{8,16},{16,24},{24,28},{28,20},{20,12},{12,4},{4,0},{1,9},{9... | collective-permute-start | bytes 442376 | tf_op jit(solution)/shard_map/ppermute | solution.py:296
  19.0 6.7 %collective-permute-start.8 = (f32[288,128]{1,0:T(8,128)S(1)}, f32[288,128]{1,0:T(8,128)S(1)}, u32[]{:S(2)}, u32[]{:S(2)}) collective-permute-start(f32[288,128]{1,0:T(8,128)S(1)} %collective-permute-done.4), channel_id=1, source_target_pairs={{0,4},{8,0},{16,8},{24,16},{28,24},{20,28},{12,20},{4,12},{1,5},{9... | collective-permute-start | bytes 442376 | tf_op jit(solution)/shard_map/ppermute | solution.py:296
  20.1 6.7 %collective-permute-start.7 = (f32[288,128]{1,0:T(8,128)S(1)}, f32[288,128]{1,0:T(8,128)S(1)}, u32[]{:S(2)}, u32[]{:S(2)}) collective-permute-start(f32[288,128]{1,0:T(8,128)S(1)} %collective-permute-done.3), channel_id=1, source_target_pairs={{0,8},{8,16},{16,24},{24,28},{28,20},{20,12},{12,4},{4,0},{1,9},{9... | collective-permute-start | bytes 442376 | tf_op jit(solution)/shard_map/ppermute | solution.py:296
  22.2 6.7 %collective-permute-start.6 = (f32[288,128]{1,0:T(8,128)S(1)}, f32[288,128]{1,0:T(8,128)S(1)}, u32[]{:S(2)}, u32[]{:S(2)}) collective-permute-start(f32[288,128]{1,0:T(8,128)S(1)} %collective-permute-done.2), channel_id=1, source_target_pairs={{0,4},{8,0},{16,8},{24,16},{28,24},{20,28},{12,20},{4,12},{1,5},{9... | collective-permute-start | bytes 442376 | tf_op jit(solution)/shard_map/ppermute | solution.py:296
  23.1 6.9 %collective-permute-start.5 = (f32[288,128]{1,0:T(8,128)S(1)}, f32[288,128]{1,0:T(8,128)S(1)}, u32[]{:S(2)}, u32[]{:S(2)}) collective-permute-start(f32[288,128]{1,0:T(8,128)S(1)} %collective-permute-done.1), channel_id=1, source_target_pairs={{0,8},{8,16},{16,24},{24,28},{28,20},{20,12},{12,4},{4,0},{1,9},{9... | collective-permute-start | bytes 442376 | tf_op jit(solution)/shard_map/ppermute | solution.py:296
  26.8 10.0 %collective-permute-start.11 = (f32[288,128]{1,0:T(8,128)S(1)}, f32[288,128]{1,0:T(8,128)S(1)}, u32[]{:S(2)}, u32[]{:S(2)}) collective-permute-start(f32[288,128]{1,0:T(8,128)S(1)} %collective-permute-done.7), channel_id=1, source_target_pairs={{0,8},{8,16},{16,24},{24,28},{28,20},{20,12},{12,4},{4,0},{1,9},{9... | collective-permute-start | bytes 442376 | tf_op jit(solution)/shard_map/ppermute | solution.py:296
  28.9 7.9 %collective-permute-start.10 = (f32[288,128]{1,0:T(8,128)S(1)}, f32[288,128]{1,0:T(8,128)S(1)}, u32[]{:S(2)}, u32[]{:S(2)}) collective-permute-start(f32[288,128]{1,0:T(8,128)S(1)} %collective-permute-done.6), channel_id=1, source_target_pairs={{0,4},{8,0},{16,8},{24,16},{28,24},{20,28},{12,20},{4,12},{1,5},{9... | collective-permute-start | bytes 442376 | tf_op jit(solution)/shard_map/ppermute | solution.py:296
  30.0 6.8 %collective-permute-start.9 = (f32[288,128]{1,0:T(8,128)S(1)}, f32[288,128]{1,0:T(8,128)S(1)}, u32[]{:S(2)}, u32[]{:S(2)}) collective-permute-start(f32[288,128]{1,0:T(8,128)S(1)} %collective-permute-done.5), channel_id=1, source_target_pairs={{0,8},{8,16},{16,24},{24,28},{28,20},{20,12},{12,4},{4,0},{1,9},{9... | collective-permute-start | bytes 442376 | tf_op jit(solution)/shard_map/ppermute | solution.py:296
  32.5 9.5 %collective-permute-start.14 = (f32[288,128]{1,0:T(8,128)S(1)}, f32[288,128]{1,0:T(8,128)S(1)}, u32[]{:S(2)}, u32[]{:S(2)}) collective-permute-start(f32[288,128]{1,0:T(8,128)S(1)} %collective-permute-done.12), channel_id=1, source_target_pairs={{0,4},{8,0},{16,8},{24,16},{28,24},{20,28},{12,20},{4,12},{1,5},{9... | collective-permute-start | bytes 442376 | tf_op jit(solution)/shard_map/ppermute | solution.py:296
  64.0 9.5 %collective-permute-start.15 = (f32[2,576,128]{2,1,0:T(8,128)}, f32[2,576,128]{2,1,0:T(8,128)S(1)}, u32[]{:S(2)}, u32[]{:S(2)}) collective-permute-start(f32[2,576,128]{2,1,0:T(8,128)} %get-tuple-element.52), channel_id=1, source_target_pairs={{0,1},{1,0},{2,3},{3,2},{4,5},{5,4},{6,7},{7,6},{8,9},{9,8},{10,11... | collective-permute-start | bytes 1769480 | tf_op jit(solution)/shard_map/ppermute | solution.py:285
  64.1 9.4 %collective-permute-start.20 = (f32[576,128]{1,0:T(8,128)S(1)}, f32[576,128]{1,0:T(8,128)S(1)}, u32[]{:S(2)}, u32[]{:S(2)}) collective-permute-start(f32[576,128]{1,0:T(8,128)S(1)} %select_select_fusion), channel_id=1, source_target_pairs={{0,2},{1,3},{2,0},{3,1},{4,6},{5,7},{6,4},{7,5},{8,10},{9,11},{10,... | collective-permute-start | bytes 884744 | tf_op jit(solution)/shard_map/ppermute | solution.py:289
  76.0 12.3 %collective-permute-start.44 = (f32[128,128]{1,0:T(8,128)S(1)}, f32[128,128]{1,0:T(8,128)S(1)}, u32[]{:S(2)}, u32[]{:S(2)}) collective-permute-start(f32[128,128]{1,0:T(8,128)S(1)} %convolution_add_fusion.1), channel_id=1, source_target_pairs={{0,3},{1,2},{2,1},{3,0},{4,7},{5,6},{6,5},{7,4},{8,11},{9,10},{10,... | collective-permute-start | bytes 196616 | tf_op jit(solution)/shard_map/ppermute | solution.py:332
  76.1 16.4 %collective-permute-start.43 = (f32[128,128]{1,0:T(8,128)S(1)}, f32[128,128]{1,0:T(8,128)S(1)}, u32[]{:S(2)}, u32[]{:S(2)}) collective-permute-start(f32[128,128]{1,0:T(8,128)S(1)} %convolution_add_fusion.1), channel_id=1, source_target_pairs={{0,2},{1,3},{2,0},{3,1},{4,6},{5,7},{6,4},{7,5},{8,10},{9,11},{10,... | collective-permute-start | bytes 196616 | tf_op jit(solution)/shard_map/ppermute | solution.py:332
  83.3 9.3 %collective-permute-start.42 = (f32[128,128]{1,0:T(8,128)S(1)}, f32[128,128]{1,0:T(8,128)S(1)}, u32[]{:S(2)}, u32[]{:S(2)}) collective-permute-start(f32[128,128]{1,0:T(8,128)S(1)} %convolution_add_fusion.1), channel_id=1, source_target_pairs={{0,1},{1,0},{2,3},{3,2},{4,5},{5,4},{6,7},{7,6},{8,9},{9,8},{10,11... | collective-permute-start | bytes 196616 | tf_op jit(solution)/shard_map/ppermute | solution.py:332
  84.2 9.7 %collective-permute-start.16 = (f32[576,128]{1,0:T(8,128)S(1)}, f32[576,128]{1,0:T(8,128)S(1)}, u32[]{:S(2)}, u32[]{:S(2)}) collective-permute-start(f32[576,128]{1,0:T(8,128)S(1)} %get-tuple-element.77), channel_id=1, source_target_pairs={{0,8},{1,12},{2,0},{3,4},{4,9},{5,13},{6,1},{7,5},{8,10},{9,14},{1... | collective-permute-start | bytes 884744 | tf_op jit(solution)/shard_map/ppermute | solution.py:282
  84.2 9.7 %collective-permute-start.17 = (f32[576,128]{1,0:T(8,128)S(1)}, f32[576,128]{1,0:T(8,128)S(1)}, u32[]{:S(2)}, u32[]{:S(2)}) collective-permute-start(f32[576,128]{1,0:T(8,128)S(1)} %get-tuple-element.62), channel_id=1, source_target_pairs={{0,0},{1,4},{2,8},{3,12},{4,1},{5,5},{6,9},{7,13},{8,2},{9,6},{10,... | collective-permute-start | bytes 884744 | tf_op jit(solution)/shard_map/ppermute | solution.py:282
  88.4 20.8 %collective-permute-start.19 = (f32[576,128]{1,0:T(8,128)S(1)}, f32[576,128]{1,0:T(8,128)S(1)}, u32[]{:S(2)}, u32[]{:S(2)}) collective-permute-start(f32[576,128]{1,0:T(8,128)S(1)} %select_select_fusion), channel_id=1, source_target_pairs={{0,1},{1,0},{2,3},{3,2},{4,5},{5,4},{6,7},{7,6},{8,9},{9,8},{10,11... | collective-permute-start | bytes 884744 | tf_op jit(solution)/shard_map/ppermute | solution.py:285
  92.5 12.7 %collective-permute-start.21 = (f32[576,128]{1,0:T(8,128)S(1)}, f32[576,128]{1,0:T(8,128)S(1)}, u32[]{:S(2)}, u32[]{:S(2)}) collective-permute-start(f32[576,128]{1,0:T(8,128)S(1)} %collective-permute-done.20), channel_id=1, source_target_pairs={{0,1},{1,0},{2,3},{3,2},{4,5},{5,4},{6,7},{7,6},{8,9},{9,8},{10,11... | collective-permute-start | bytes 884744 | tf_op jit(solution)/shard_map/ppermute | solution.py:285
  94.2 8.9 %collective-permute-start.18 = (f32[288,128]{1,0:T(8,128)S(1)}, f32[288,128]{1,0:T(8,128)S(1)}, u32[]{:S(2)}, u32[]{:S(2)}) collective-permute-start(f32[288,128]{1,0:T(8,128)S(1)} %get-tuple-element.79), channel_id=1, source_target_pairs={{0,8},{8,16},{16,24},{24,28},{28,20},{20,12},{12,4},{4,0},{1,9},{9... | collective-permute-start | bytes 442376 | tf_op jit(solution)/shard_map/ppermute | solution.py:296
  98.5 10.9 %collective-permute-start.30 = (f32[288,128]{1,0:T(8,128)S(1)}, f32[288,128]{1,0:T(8,128)S(1)}, u32[]{:S(2)}, u32[]{:S(2)}) collective-permute-start(f32[288,128]{1,0:T(8,128)S(1)} %get-tuple-element.78), channel_id=1, source_target_pairs={{0,4},{8,0},{16,8},{24,16},{28,24},{20,28},{12,20},{4,12},{1,5},{9... | collective-permute-start | bytes 442376 | tf_op jit(solution)/shard_map/ppermute | solution.py:296
  103.1 8.5 %collective-permute-start.28 = (f32[288,128]{1,0:T(8,128)S(1)}, f32[288,128]{1,0:T(8,128)S(1)}, u32[]{:S(2)}, u32[]{:S(2)}) collective-permute-start(f32[288,128]{1,0:T(8,128)S(1)} %get-tuple-element.79), channel_id=1, source_target_pairs={{0,4},{8,0},{16,8},{24,16},{28,24},{20,28},{12,20},{4,12},{1,5},{9... | collective-permute-start | bytes 442376 | tf_op jit(solution)/shard_map/ppermute | solution.py:296
  105.1 9.9 %collective-permute-start.22 = (f32[576,128]{1,0:T(8,128)S(1)}, f32[576,128]{1,0:T(8,128)S(1)}, u32[]{:S(2)}, u32[]{:S(2)}) collective-permute-start(f32[576,128]{1,0:T(8,128)S(1)} %get-tuple-element.62), channel_id=1, source_target_pairs={{0,2},{1,3},{2,0},{3,1},{4,6},{5,7},{6,4},{7,5},{8,10},{9,11},{10,... | collective-permute-start | bytes 884744 | tf_op jit(solution)/shard_map/ppermute | solution.py:289
  109.4 11.3 %collective-permute-start.33 = (f32[288,128]{1,0:T(8,128)S(1)}, f32[288,128]{1,0:T(8,128)S(1)}, u32[]{:S(2)}, u32[]{:S(2)}) collective-permute-start(f32[288,128]{1,0:T(8,128)S(1)} %collective-permute-done.30), channel_id=1, source_target_pairs={{0,4},{8,0},{16,8},{24,16},{28,24},{20,28},{12,20},{4,12},{1,5},{9... | collective-permute-start | bytes 442376 | tf_op jit(solution)/shard_map/ppermute | solution.py:296
  109.5 11.5 %collective-permute-start.32 = (f32[288,128]{1,0:T(8,128)S(1)}, f32[288,128]{1,0:T(8,128)S(1)}, u32[]{:S(2)}, u32[]{:S(2)}) collective-permute-start(f32[288,128]{1,0:T(8,128)S(1)} %collective-permute-done.29), channel_id=1, source_target_pairs={{0,8},{8,16},{16,24},{24,28},{28,20},{20,12},{12,4},{4,0},{1,9},{9... | collective-permute-start | bytes 442376 | tf_op jit(solution)/shard_map/ppermute | solution.py:296
  111.6 11.1 %collective-permute-start.31 = (f32[288,128]{1,0:T(8,128)S(1)}, f32[288,128]{1,0:T(8,128)S(1)}, u32[]{:S(2)}, u32[]{:S(2)}) collective-permute-start(f32[288,128]{1,0:T(8,128)S(1)} %collective-permute-done.28), channel_id=1, source_target_pairs={{0,4},{8,0},{16,8},{24,16},{28,24},{20,28},{12,20},{4,12},{1,5},{9... | collective-permute-start | bytes 442376 | tf_op jit(solution)/shard_map/ppermute | solution.py:296
  115.1 18.2 %collective-permute-start.26 = (f32[576,128]{1,0:T(8,128)S(1)}, f32[576,128]{1,0:T(8,128)S(1)}, u32[]{:S(2)}, u32[]{:S(2)}) collective-permute-start(f32[576,128]{1,0:T(8,128)S(1)} %fusion.25), channel_id=1, source_target_pairs={{0,2},{1,3},{2,0},{3,1},{4,6},{5,7},{6,4},{7,5},{8,10},{9,11},{10,... | collective-permute-start | bytes 884744 | tf_op jit(solution)/shard_map/ppermute | solution.py:289
  120.7 10.4 %collective-permute-start.36 = (f32[288,128]{1,0:T(8,128)S(1)}, f32[288,128]{1,0:T(8,128)S(1)}, u32[]{:S(2)}, u32[]{:S(2)}) collective-permute-start(f32[288,128]{1,0:T(8,128)S(1)} %collective-permute-done.33), channel_id=1, source_target_pairs={{0,4},{8,0},{16,8},{24,16},{28,24},{20,28},{12,20},{4,12},{1,5},{9... | collective-permute-start | bytes 442376 | tf_op jit(solution)/shard_map/ppermute | solution.py:296
  121.0 12.2 %collective-permute-start.35 = (f32[288,128]{1,0:T(8,128)S(1)}, f32[288,128]{1,0:T(8,128)S(1)}, u32[]{:S(2)}, u32[]{:S(2)}) collective-permute-start(f32[288,128]{1,0:T(8,128)S(1)} %collective-permute-done.32), channel_id=1, source_target_pairs={{0,8},{8,16},{16,24},{24,28},{28,20},{20,12},{12,4},{4,0},{1,9},{9... | collective-permute-start | bytes 442376 | tf_op jit(solution)/shard_map/ppermute | solution.py:296
  122.7 8.5 %collective-permute-start.34 = (f32[288,128]{1,0:T(8,128)S(1)}, f32[288,128]{1,0:T(8,128)S(1)}, u32[]{:S(2)}, u32[]{:S(2)}) collective-permute-start(f32[288,128]{1,0:T(8,128)S(1)} %collective-permute-done.31), channel_id=1, source_target_pairs={{0,4},{8,0},{16,8},{24,16},{28,24},{20,28},{12,20},{4,12},{1,5},{9... | collective-permute-start | bytes 442376 | tf_op jit(solution)/shard_map/ppermute | solution.py:296
  (23 other events, 233.4 us)
